TPU v7x, 512 devices: a whole 4x4x16 slice. The times are simulated.
512 devices in a mesh: ctx: 64 (over z_hi, x, y), head: 8 (over z_lo, core).
Axes of the slice: x: 4, y: 4, z: 16 (z_hi: 4, z_lo: 4; z = z_hi * 4 + z_lo), core: 2. Of those that a mesh axis runs over, the one named last changes fastest.
Arguments:
- queries: bfloat16 [16384, 6144], P(('ctx', 'head')), may hold values from -32 to 32
- keys: bfloat16 [16384, 6144], P(('ctx', 'head')), may hold values from -12 to 12
- values: bfloat16 [16384, 6144], P(('ctx', 'head')), may hold values from -6 to 6
- cache_keys: bfloat16 [32768, 6144], P('ctx', 'head'), may hold values from -6 to 6
- cache_values: bfloat16 [32768, 6144], P('ctx', 'head'), may hold values from -6 to 6
- pattern: int32 [128, 4], replicated, may hold values from 0 to 255, as said below
- reached: int32 [128], replicated, may hold values from 1 to 4, as said below
- gate: float32 [6144], replicated, may hold values from 0.5 to 2
Outputs:
- mixed: bfloat16 [16384, 6144], P(('ctx', 'head'))
Inputs may be any that keep to these rules, and one draw needn't show every extreme that they name: `pattern`: every entry of row g names a cached tile of ctx index g // 2 - 1, g // 2 or g // 2 + 1, where ctx index c holds cached tiles c * 4 to (c + 1) * 4 - 1. Only the first reached[g] entries of row g of pattern are used.
All inputs are finite; a program needn't handle non-finite values.
Results may differ from a plain program's by a relative error of at most 0.011.
Values may be sent and summed in bfloat16 or wider, within the bound.
No kernel may reach another device: no remote copies, remote signals or barrier semaphores. Data moves between devices by JAX's collectives and lax.ppermute only.
A program may use at most 64 MiB of HBM per device.

v0:
```python
import jax
import jax.numpy as jnp
from jax import lax
from jax.sharding import PartitionSpec as P

HD = 128
TILE = 128
REACH = 4


NEGATIVE = -1e30


def with_halo(block, sides, width):
    for axis, dim in sides:
        count = lax.axis_size(axis)
        forward = [(i, i + 1) for i in range(count - 1)]
        backward = [(target, source) for source, target in forward]
        low = lax.ppermute(
            lax.slice_in_dim(block, block.shape[dim] - width, None, axis=dim), axis, forward
        )
        high = lax.ppermute(lax.slice_in_dim(block, 0, width, axis=dim), axis, backward)
        block = jnp.concatenate([low, block, high], axis=dim)
    return block


def tile_attend(q_tile, key_blocks, value_blocks, usable_keys):
    scores = jnp.einsum(
        "qhd,nkhd->hqnk", q_tile, key_blocks, preferred_element_type=jnp.float32
    ) * q_tile.shape[2] ** (-0.5)
    keep_mask = usable_keys[None, None, :, None]
    scores = jnp.where(keep_mask, scores, NEGATIVE)
    row_peak = jnp.max(scores, axis=(2, 3))
    expos = jnp.exp(scores - row_peak[:, :, None, None])
    row_total = jnp.sum(expos, axis=(2, 3))
    weights = expos.astype(jnp.bfloat16)
    summed = jnp.einsum("hqnk,nkhd->qhd", weights, value_blocks, preferred_element_type=jnp.float32)
    return (summed, row_peak, row_total)


def finish(portions):
    overall_peak = portions[0][1]
    numerator = 0.0
    denominator = 0.0
    for portion in portions:
        factor = jnp.exp(portion[1] - overall_peak)
        denominator = denominator + factor * portion[2]
        numerator = numerator + portion[0] * jnp.transpose(factor, (0, 2, 1))[..., None]
    return numerator / jnp.transpose(denominator, (0, 2, 1))[..., None]


def local(queries, keys, values, cache_keys, cache_values, pattern, reached, gate):
    local_q, local_k, local_v = (
        lax.all_to_all(queries, "head", split_axis=1, concat_axis=0, tiled=True),
        lax.all_to_all(keys, "head", split_axis=1, concat_axis=0, tiled=True),
        lax.all_to_all(values, "head", split_axis=1, concat_axis=0, tiled=True),
    )
    rows = local_q.shape[0]
    width = local_q.shape[1]
    heads_here = width // HD
    tiles_here = rows // TILE
    ctx_count = lax.axis_size("ctx")
    ctx_index = lax.axis_index("ctx")
    all_tiles = ctx_count * tiles_here
    first_tile = ctx_index * tiles_here
    cache_tiles = cache_keys.shape[0] // TILE
    rim_blocks = with_halo(jnp.stack([local_k, local_v]), (("ctx", 1),), 2 * TILE)
    tile_ids = first_tile + jnp.arange(tiles_here, dtype=jnp.int32)
    near_ids = tile_ids[:, None] + jnp.arange(-2, 3, dtype=jnp.int32)[None, :]
    group_valid = (near_ids >= 0) & (near_ids < all_tiles)
    own_pattern = lax.dynamic_slice_in_dim(pattern, first_tile, tiles_here, 0)
    own_reached = lax.dynamic_slice_in_dim(reached, first_tile, tiles_here, 0)
    slot_ids = jnp.arange(REACH, dtype=jnp.int32)
    cache_stack = jnp.stack([cache_keys, cache_values])

    def query_tile(block_q, tile_index):
        return lax.dynamic_slice_in_dim(block_q, tile_index * TILE, TILE, 0).reshape(
            TILE, heads_here, HD
        )

    def group_blocks(tile_index):
        window = lax.dynamic_slice_in_dim(rim_blocks, tile_index * TILE, 5 * TILE, 1)
        return window.reshape(2, 5, TILE, heads_here, HD)

    widened = with_halo(cache_stack, (("ctx", 1),), cache_keys.shape[0])
    widened = widened.reshape(2, 3 * cache_tiles, TILE, heads_here, HD)

    def one_tile(tile_index):
        local_ids = own_pattern[tile_index] - (ctx_index - 1) * cache_tiles
        picked = jnp.take(widened, local_ids, axis=1)
        blocks = jnp.concatenate([group_blocks(tile_index), picked], axis=1)
        usable_keys = jnp.concatenate([group_valid[tile_index], slot_ids < own_reached[tile_index]])
        return tile_attend(query_tile(local_q, tile_index), blocks[0], blocks[1], usable_keys)

    attended = finish([lax.map(one_tile, jnp.arange(tiles_here, dtype=jnp.int32))])
    gate_part = lax.dynamic_slice_in_dim(gate, lax.axis_index("head") * width, width, 0)
    gated = (attended.reshape(rows, width) * gate_part).astype(jnp.bfloat16)
    return lax.all_to_all(gated, "head", split_axis=0, concat_axis=1, tiled=True)


def solution(mesh):
    placed = (
        P(("ctx", "head"), None),
        P(("ctx", "head"), None),
        P(("ctx", "head"), None),
        P("ctx", "head"),
        P("ctx", "head"),
        P(),
        P(),
        P(),
    )
    return jax.shard_map(
        local, mesh=mesh, in_specs=placed, out_specs=P(("ctx", "head"), None), check_vma=False
    )
```

profile of v0, /device:TPU:256, one launch (start us, length us, event | category | flops | bytes accessed | tf_op | source)
XLA Modules:
  0.0 328.4 jit_solution(431748586827617101)
XLA Ops:
  0.0 1.9 copy.82
  1.9 3.6 %all-to-all-start = ((bf16[32,8,768]{2,0,1:T(8,128)(2,1)}), bf16[32,8,768]{2,0,1:T(8,128)(2,1)S(1)}, u32[]{:S(2)}, u32[]{:S(2)}) async-start(bf16[32,8,768]{2,0,1:T(8,128)(2,1)} %bitcast.70), calls=%async_computation | async-start | bytes 786432 | tf_op jit(solution)/shard_map/all_to_all | solution.py:55
  5.5 1.8 copy.81
  7.3 10.7 %all-to-all-done = bf16[32,8,768]{2,0,1:T(8,128)(2,1)S(1)} async-done(((bf16[32,8,768]{2,0,1:T(8,128)(2,1)}), bf16[32,8,768]{2,0,1:T(8,128)(2,1)S(1)}, u32[]{:S(2)}, u32[]{:S(2)}) %all-to-all-start) | async-done | bytes 393248 | tf_op jit(solution)/shard_map/all_to_all | solution.py:55
  18.0 3.5 %all-to-all-start.1 = ((bf16[32,8,768]{2,0,1:T(8,128)(2,1)}), bf16[32,8,768]{2,0,1:T(8,128)(2,1)S(1)}, u32[]{:S(2)}, u32[]{:S(2)}) async-start(bf16[32,8,768]{2,0,1:T(8,128)(2,1)} %bitcast.69), calls=%async_computation.1 | async-start | bytes 786432 | tf_op jit(solution)/shard_map/all_to_all | solution.py:56
  21.5 1.3 pad_maximum_fusion.3
  22.8 3.5 %collective-permute-start.2 = (bf16[2,512,768]{2,1,0:T(8,128)(2,1)}, bf16[2,512,768]{2,1,0:T(8,128)(2,1)}, u32[]{:S(2)}, u32[]{:S(2)}) collective-permute-start(bf16[2,512,768]{2,1,0:T(8,128)(2,1)} %pad_maximum_fusion.3), channel_id=1, source_target_pairs={{0,8},{8,16},{16,24},{24,32},{32,40},{40,48},{48,56},{56,64},{64,7... | collective-permute-start | bytes 4718600 | tf_op jit(solution)/shard_map/ppermute | solution.py:19
  26.2 10.5 %collective-permute-start.3 = (bf16[2,512,768]{2,1,0:T(8,128)(2,1)}, bf16[2,512,768]{2,1,0:T(8,128)(2,1)}, u32[]{:S(2)}, u32[]{:S(2)}) collective-permute-start(bf16[2,512,768]{2,1,0:T(8,128)(2,1)} %pad_maximum_fusion.3), channel_id=1, source_target_pairs={{8,0},{16,8},{24,16},{32,24},{40,32},{48,40},{56,48},{64,56},{72,6... | collective-permute-start | bytes 4718600 | tf_op jit(solution)/shard_map/ppermute | solution.py:22
  36.8 0.8 copy.80
  37.5 5.0 %all-to-all-start.2 = ((bf16[32,8,768]{2,0,1:T(8,128)(2,1)}), bf16[32,8,768]{2,0,1:T(8,128)(2,1)S(1)}, u32[]{:S(2)}, u32[]{:S(2)}) async-start(bf16[32,8,768]{2,0,1:T(8,128)(2,1)} %bitcast.68), calls=%async_computation.2 | async-start | bytes 786432 | tf_op jit(solution)/shard_map/all_to_all | solution.py:54
  42.8 0.8 dynamic_slice.42
  43.6 1.0 pad_maximum_fusion.4
  44.6 1.9 collective-permute-start
  46.5 37.1 %collective-permute-start.1 = (bf16[2,256,768]{2,1,0:T(8,128)(2,1)}, bf16[2,256,768]{2,1,0:T(8,128)(2,1)}, u32[]{:S(2)}, u32[]{:S(2)}) collective-permute-start(bf16[2,256,768]{2,1,0:T(8,128)(2,1)} %pad_maximum_fusion.4), channel_id=1, source_target_pairs={{8,0},{16,8},{24,16},{32,24},{40,32},{48,40},{56,48},{64,56},{72,6... | collective-permute-start | bytes 2359304 | tf_op jit(solution)/shard_map/ppermute | solution.py:22
  83.7 128.9 %collective-permute-done.3 = bf16[2,512,768]{2,1,0:T(8,128)(2,1)} collective-permute-done((bf16[2,512,768]{2,1,0:T(8,128)(2,1)}, bf16[2,512,768]{2,1,0:T(8,128)(2,1)}, u32[]{:S(2)}, u32[]{:S(2)}) %collective-permute-start.3) | collective-permute-done | bytes 1572896 | tf_op jit(solution)/shard_map/ppermute | solution.py:22
  212.6 4.9 %pad_maximum_fusion.1 = bf16[2,1536,768]{2,1,0:T(8,128)(2,1)} fusion(bf16[2,512,768]{2,1,0:T(8,128)(2,1)} %collective-permute-done.3, bf16[1,512,768]{2,1,0:T(8,128)(2,1)S(1)} %bitcast.112, bf16[1,512,768]{2,1,0:T(8,128)(2,1)S(1)} %bitcast.114, bf16[2,512,768]{2,1,0:T(8,128)(2,1)} %collective-permute-done.2), kind=kLoop, calls=%fused_computation.38 | loop fusion | flops 18874368 | bytes 9437184 | tf_op jit(solution)/shard_map/concatenate | solution.py:23
  217.5 10.8 %reshape.82 = bf16[2,12,128,6,128]{4,3,2,1,0:T(8,128)(2,1)} reshape(bf16[2,1536,768]{2,1,0:T(8,128)(2,1)} %pad_maximum_fusion.1) | data formatting | bytes 9437184 | tf_op jit(solution)/shard_map/reshape | solution.py:86
  228.3 6.4 %copy.60 = bf16[2,12,128,6,128]{4,2,3,1,0:T(8,128)(2,1)} copy(bf16[2,12,128,6,128]{4,3,2,1,0:T(8,128)(2,1)} %reshape.82) | data formatting | bytes 9437184
  234.7 13.2 %collective-permute-done = bf16[2,256,768]{2,1,0:T(8,128)(2,1)} collective-permute-done((bf16[2,256,768]{2,1,0:T(8,128)(2,1)}, bf16[2,256,768]{2,1,0:T(8,128)(2,1)}, u32[]{:S(2)}, u32[]{:S(2)}) %collective-permute-start) | collective-permute-done | bytes 786464 | tf_op jit(solution)/shard_map/ppermute | solution.py:19
  247.9 3.0 pad_maximum_fusion.2
  250.9 47.6 %while.17 = (s32[]{:T(128)}, f32[2,128,6,128]{1,3,2,0:T(8,128)}, f32[2,6,128]{2,1,0:T(8,128)S(1)}, f32[2,6,128]{2,1,0:T(8,128)S(1)}, s32[2]{0:T(128)S(1)}, /*ind...) while((s32[]{:T(128)}, f32[2,128,6,128]{1,3,2,0:T(8,128)}, ...), condition=%wide.region_3.4_spmd.clone, body=%wide.region_0.3_spmd.clone.sunk | while | flops 465272384 | bytes 78874744 | solution.py:95
  250.9 0.7 dynamic_slice.72
  253.6 3.2 gather_fusion
  256.8 1.4 fusion.49
  258.9 2.9 constant_dynamic-slice_fusion.6
  261.9 4.2 %reshape.105 = bf16[2,5,128,6,128]{4,3,2,1,0:T(8,128)(2,1)S(1)} reshape(bf16[2,640,768]{2,1,0:T(8,128)(2,1)} %constant_dynamic-slice_fusion.6) | data formatting | bytes 3932160 | tf_op jit(solution)/shard_map/while/body/eval_jaxpr/reshape | solution.py:83
  266.1 0.5 copy.87
  266.6 1.3 copy-done.1
  267.9 0.2 pad_maximum_fusion.6
  268.1 0.2 copy.88
  268.2 0.6 fusion.50
  268.8 0.7 dynamic_slice.73
  269.5 0.7 iota_compare_fusion.2
  270.3 0.5 fusion.51
  270.8 0.8 fusion.53
  271.6 0.2 copy-done.2
  271.8 0.5 copy-done.4
  272.3 0.2 copy-done.7
  272.5 1.4 fusion.52
  273.8 0.9 copy-done.8
  274.7 0.6 dynamic_slice.72
  277.4 3.2 gather_fusion
  280.6 1.4 fusion.49
  282.7 2.9 constant_dynamic-slice_fusion.6
  285.7 4.2 %reshape.105 = bf16[2,5,128,6,128]{4,3,2,1,0:T(8,128)(2,1)S(1)} reshape(bf16[2,640,768]{2,1,0:T(8,128)(2,1)} %constant_dynamic-slice_fusion.6) | data formatting | bytes 3932160 | tf_op jit(solution)/shard_map/while/body/eval_jaxpr/reshape | solution.py:83
  289.9 0.5 copy.87
  290.4 1.3 copy-done.1
  291.7 0.2 pad_maximum_fusion.6
  291.9 0.2 copy.88
  292.0 0.6 fusion.50
  292.6 0.7 dynamic_slice.73
  293.3 0.7 iota_compare_fusion.2
  294.1 0.5 fusion.51
  294.6 0.8 fusion.53
  295.4 0.2 copy-done.2
  295.6 0.5 copy-done.4
  296.1 0.2 copy-done.7
  296.3 1.4 fusion.52
  297.7 0.9 copy-done.8
  298.5 1.2 multiply_divide_fusion
  299.7 0.4 copy.62
  300.1 0.2 reshape.83
  300.4 27.2 %all_to_all.67 = bf16[8,32,768]{2,1,0:T(8,128)(2,1)S(1)} all-to-all(bf16[8,32,768]{2,1,0:T(8,128)(2,1)S(1)} %multiply_convert_fusion), channel_id=1, replica_groups=mesh['ctx'=64,'head'=8] {'head'}, dimensions={0} | all-to-all | bytes 786432 | tf_op jit(solution)/shard_map/all_to_all | solution.py:98
  327.6 0.8 copy.73
  (54 shorter events, 0.7 us)
Async XLA Ops:
  0.0 42.5 %copy-start = (s32[128,4]{0,1:T(4,128)S(1)}, s32[128,4]{0,1:T(4,128)}, u32[]{:S(2)}) copy-start(s32[128,4]{0,1:T(4,128)} %param.15) | copy-start | bytes 6148
  0.0 21.4 %copy-start.6 = (bf16[512,768]{1,0:T(8,128)(2,1)S(1)}, bf16[512,768]{1,0:T(8,128)(2,1)}, u32[]{:S(2)}) copy-start(bf16[512,768]{1,0:T(8,128)(2,1)} %param.13) | copy-start | bytes 2359300
  0.0 21.4 %copy-start.5 = (bf16[512,768]{1,0:T(8,128)(2,1)S(1)}, bf16[512,768]{1,0:T(8,128)(2,1)}, u32[]{:S(2)}) copy-start(bf16[512,768]{1,0:T(8,128)(2,1)} %param.14) | copy-start | bytes 2359300
  0.0 36.7 %copy-start.9 = (bf16[32,6144]{1,0:T(8,128)(2,1)S(1)}, bf16[32,6144]{1,0:T(8,128)(2,1)}, u32[]{:S(2)}) copy-start(bf16[32,6144]{1,0:T(8,128)(2,1)} %param.10) | copy-start | bytes 1179652
  1.9 40.8 %copy-start.10 = (s32[128]{0:T(128)S(1)}, s32[128]{0:T(128)}, u32[]{:S(2)}) copy-start(s32[128]{0:T(128)} %param.16) | copy-start | bytes 1540
  1.9 16.0 %all-to-all-start = ((bf16[32,8,768]{2,0,1:T(8,128)(2,1)}), bf16[32,8,768]{2,0,1:T(8,128)(2,1)S(1)}, u32[]{:S(2)}, u32[]{:S(2)}) async-start(bf16[32,8,768]{2,0,1:T(8,128)(2,1)} %bitcast.70), calls=%async_computation | async-start | bytes 786432 | tf_op jit(solution)/shard_map/all_to_all | solution.py:55
  18.0 19.5 %all-to-all-start.1 = ((bf16[32,8,768]{2,0,1:T(8,128)(2,1)}), bf16[32,8,768]{2,0,1:T(8,128)(2,1)S(1)}, u32[]{:S(2)}, u32[]{:S(2)}) async-start(bf16[32,8,768]{2,0,1:T(8,128)(2,1)} %bitcast.69), calls=%async_computation.1 | async-start | bytes 786432 | tf_op jit(solution)/shard_map/all_to_all | solution.py:56
  22.8 60.9 %collective-permute-start.2 = (bf16[2,512,768]{2,1,0:T(8,128)(2,1)}, bf16[2,512,768]{2,1,0:T(8,128)(2,1)}, u32[]{:S(2)}, u32[]{:S(2)}) collective-permute-start(bf16[2,512,768]{2,1,0:T(8,128)(2,1)} %pad_maximum_fusion.3), channel_id=1, source_target_pairs={{0,8},{8,16},{16,24},{24,32},{32,40},{40,48},{48,56},{56,64},{64,7... | collective-permute-start | bytes 4718600 | tf_op jit(solution)/shard_map/ppermute | solution.py:19
  26.2 186.4 %collective-permute-start.3 = (bf16[2,512,768]{2,1,0:T(8,128)(2,1)}, bf16[2,512,768]{2,1,0:T(8,128)(2,1)}, u32[]{:S(2)}, u32[]{:S(2)}) collective-permute-start(bf16[2,512,768]{2,1,0:T(8,128)(2,1)} %pad_maximum_fusion.3), channel_id=1, source_target_pairs={{8,0},{16,8},{24,16},{32,24},{40,32},{48,40},{56,48},{64,56},{72,6... | collective-permute-start | bytes 4718600 | tf_op jit(solution)/shard_map/ppermute | solution.py:22
  37.5 213.4 %all-to-all-start.2 = ((bf16[32,8,768]{2,0,1:T(8,128)(2,1)}), bf16[32,8,768]{2,0,1:T(8,128)(2,1)S(1)}, u32[]{:S(2)}, u32[]{:S(2)}) async-start(bf16[32,8,768]{2,0,1:T(8,128)(2,1)} %bitcast.68), calls=%async_computation.2 | async-start | bytes 786432 | tf_op jit(solution)/shard_map/all_to_all | solution.py:54
  44.6 203.4 %collective-permute-start = (bf16[2,256,768]{2,1,0:T(8,128)(2,1)}, bf16[2,256,768]{2,1,0:T(8,128)(2,1)}, u32[]{:S(2)}, u32[]{:S(2)}) collective-permute-start(bf16[2,256,768]{2,1,0:T(8,128)(2,1)} %pad_maximum_fusion.4), channel_id=1, source_target_pairs={{0,8},{8,16},{16,24},{24,32},{32,40},{40,48},{48,56},{56,64},{64,7... | collective-permute-start | bytes 2359304 | tf_op jit(solution)/shard_map/ppermute | solution.py:19
  46.5 201.5 %collective-permute-start.1 = (bf16[2,256,768]{2,1,0:T(8,128)(2,1)}, bf16[2,256,768]{2,1,0:T(8,128)(2,1)}, u32[]{:S(2)}, u32[]{:S(2)}) collective-permute-start(bf16[2,256,768]{2,1,0:T(8,128)(2,1)} %pad_maximum_fusion.4), channel_id=1, source_target_pairs={{8,0},{16,8},{24,16},{32,24},{40,32},{48,40},{56,48},{64,56},{72,6... | collective-permute-start | bytes 2359304 | tf_op jit(solution)/shard_map/ppermute | solution.py:22
  266.1 1.8 copy-start.3
  266.6 1.3 copy-start.1
  270.3 1.5 copy-start.2
  270.3 2.0 copy-start.4
  270.3 2.2 copy-start.7
  273.8 0.9 copy-start.8
  289.9 1.8 copy-start.3
  290.4 1.3 copy-start.1
  294.1 1.5 copy-start.2
  294.1 2.0 copy-start.4
  294.1 2.2 copy-start.7
  297.6 0.9 copy-start.8
where the time goes:
time: 330 us; the launch traced here: 328 us
  waiting for transfers between devices  153 us (46%)
  starting transfers between devices  65 us (20%)
  local copies, waits for them, and re-layouts  54.7 us (17%)
  blocking collectives  27.2 us (8%)
  other arithmetic  18.8 us (6%)
  loops' own time  5.72 us (2%)
  matrix products  3.93 us (1%)
    ppermute x2, waiting for transfers between devices, with_halo(): lax.ppermute(lax.slice_in_dim(block, 0, width, axis=dim), axis, backward)  129 us
    ppermute x2, starting transfers between devices, with_halo(): lax.ppermute(lax.slice_in_dim(block, 0, width, axis=dim), axis, backward)  47.6 us
    all_to_all x1, blocking collectives, local(): lax.all_to_all(gated, 'head', split_axis=0, concat_axis=1, tiled=True)  27.2 us
    ppermute x2, waiting for transfers between devices, with_halo(): lax.ppermute(lax.slice_in_dim(block, block.shape[dim] - width, None, axis...  13.2 us
    reshape x1, local copies, waits for them, and re-layouts, local(): widened = widened.reshape(2, 3 * cache_tiles, TILE, heads_here, HD)  10.8 us
    all_to_all x1, waiting for transfers between devices, local(): lax.all_to_all(keys, 'head', split_axis=1, concat_axis=0, tiled=True)  10.7 us
    reshape x4, local copies, waits for them, and re-layouts, group_blocks(): return window.reshape(2, 5, TILE, heads_here, HD)  9.41 us
    concatenate x2, other arithmetic, with_halo(): block = jnp.concatenate([low, block, high], axis=dim)  7.87 us
  transfers between devices with their start and end apart: 7, of which 3 were waited for; matrix products, arithmetic and copies ran while one was open for 9% of the time, Pallas kernels for 0%

commit v1 on v0

v1 whole, which is shorter than its diff:
```python
import functools
import math

import jax
import jax.numpy as jnp
from jax import lax
from jax.experimental import pallas as pl
from jax.experimental.pallas import tpu as pltpu
from jax.sharding import PartitionSpec as P

HD = 128
TILE = 128
REACH = 4
NEGATIVE = -1e30
LIMIT = 24 << 20
LOG2E = math.log2(math.e)
NT = (((1,), (1,)), ((), ()))


def vmem():
    return pl.BlockSpec(memory_space=pltpu.VMEM)


def smem():
    return pl.BlockSpec(memory_space=pltpu.SMEM)


def tile_bias(pattern_ref, reached_ref, tile, cached_id, tile_count):
    row = jnp.clip(tile, 0, tile_count - 1)
    used = reached_ref[row]
    times = jnp.int32(0)
    for slot in range(REACH):
        hit = jnp.logical_and(slot < used, pattern_ref[row, slot] == cached_id)
        times = times + jnp.where(hit, 1, 0)
    bias = jnp.where(times == 1, 0.0, NEGATIVE)
    bias = jnp.where(times == 2, 1.0, bias)
    bias = jnp.where(times == 3, math.log2(3.0), bias)
    return jnp.where(times == 4, 2.0, bias)


def fill_bias(bias_ref, pattern_ref, reached_ref, rel_tiles, own_tiles, cached_tiles):
    ctx = lax.axis_index("ctx")
    tile_count = pattern_ref.shape[0]
    for row, rel in enumerate(rel_tiles):
        for t in range(own_tiles):
            near = 0.0 if abs(rel - t) <= 2 else NEGATIVE
            bias_ref[row, :, t * TILE : (t + 1) * TILE] = jnp.full((8, TILE), near, jnp.float32)
        for u in range(cached_tiles):
            bias = tile_bias(
                pattern_ref, reached_ref, ctx * own_tiles + rel, ctx * cached_tiles + u, tile_count
            )
            at = (own_tiles + u) * TILE
            bias_ref[row, :, at : at + TILE] = jnp.full((8, TILE), bias, jnp.float32)


def attend(q, k, v, ck, cv, bias):
    scale = HD**-0.5 * LOG2E
    near = lax.dot_general(q, k, NT, preferred_element_type=jnp.float32)
    far = lax.dot_general(q, ck, NT, preferred_element_type=jnp.float32)
    split = near.shape[1]
    near = near * scale + bias[:, :split]
    far = far * scale + bias[:, split:]
    peak = jnp.maximum(
        jnp.max(near, axis=1, keepdims=True), jnp.max(far, axis=1, keepdims=True)
    )
    near = jnp.exp2(near - peak)
    far = jnp.exp2(far - peak)
    total = jnp.sum(near, axis=1, keepdims=True) + jnp.sum(far, axis=1, keepdims=True)
    out = jnp.dot(near.astype(jnp.bfloat16), v, preferred_element_type=jnp.float32)
    out = out + jnp.dot(far.astype(jnp.bfloat16), cv, preferred_element_type=jnp.float32)
    return out / total, peak + jnp.log2(total)


def pieces(lse):
    high = lse.astype(jnp.bfloat16).astype(jnp.float32)
    rest = lse - high
    middle = rest.astype(jnp.bfloat16).astype(jnp.float32)
    low = rest - middle
    return (high + pltpu.roll(middle, 32, 1) + pltpu.roll(low, 64, 1)).astype(jnp.bfloat16)


def whole(block):
    block = block.astype(jnp.float32)
    return block + pltpu.roll(block, 96, 1) + pltpu.roll(block, 64, 1)


def attend_all(q_ref, kv_ref, ck_ref, cv_ref, bias_ref, first_row, put):
    parts, _, part, width = kv_ref.shape
    rows = parts * part
    lane = lax.broadcasted_iota(jnp.int32, (TILE, HD), 1)
    for t in range(rows // TILE):
        bias = bias_ref[first_row + t, 0:1, :]
        stats = jnp.zeros((TILE, HD), jnp.float32)
        for h in range(width // HD):
            cols = slice(h * HD, (h + 1) * HD)
            q = q_ref[t * TILE : (t + 1) * TILE, cols]
            k = kv_ref[:, 0, :, cols].reshape(rows, HD)
            v = kv_ref[:, 1, :, cols].reshape(rows, HD)
            out, lse = attend(q, k, v, ck_ref[:, cols], cv_ref[:, cols], bias)
            put(t, cols, out)
            stats = jnp.where(lane == h, lse, stats)
        put(t, None, stats)


def far_kernel(
    pattern_ref, reached_ref, below_ref, above_ref, kv_ref, ck_ref, cv_ref, to_below_ref, to_above_ref, bias_ref
):
    own = kv_ref.shape[0] * kv_ref.shape[2] // TILE
    rel = tuple(range(-own, 0)) + tuple(range(own, 2 * own))
    fill_bias(bias_ref, pattern_ref, reached_ref, rel, own, ck_ref.shape[0] // TILE)
    width = kv_ref.shape[3]
    for side, (q_ref, o_ref) in enumerate(((below_ref, to_below_ref), (above_ref, to_above_ref))):

        def put(t, cols, value, o_ref=o_ref):
            rows = slice(t * TILE, (t + 1) * TILE)
            if cols is None:
                o_ref[rows, width:] = pieces(value)
            else:
                o_ref[rows, cols] = value.astype(jnp.bfloat16)

        attend_all(q_ref, kv_ref, ck_ref, cv_ref, bias_ref, side * own, put)


def own_kernel(pattern_ref, reached_ref, q_ref, kv_ref, ck_ref, cv_ref, o_ref, stats_ref, bias_ref):
    own = kv_ref.shape[0] * kv_ref.shape[2] // TILE
    fill_bias(bias_ref, pattern_ref, reached_ref, tuple(range(own)), own, ck_ref.shape[0] // TILE)

    def put(t, cols, value):
        rows = slice(t * TILE, (t + 1) * TILE)
        if cols is None:
            stats_ref[rows, :] = value
        else:
            o_ref[rows, cols] = value

    attend_all(q_ref, kv_ref, ck_ref, cv_ref, bias_ref, 0, put)


def mix_kernel(count, o_ref, stats_ref, low_ref, high_ref, gate_ref, out_ref):
    ctx = lax.axis_index("ctx")
    head = lax.axis_index("head")
    rows, width = o_ref.shape
    heads = width // HD
    mine = stats_ref[...]
    low = jnp.where(ctx > 0, whole(low_ref[:, width:]), NEGATIVE)
    high = jnp.where(ctx < count - 1, whole(high_ref[:, width:]), NEGATIVE)
    peak = jnp.maximum(jnp.maximum(mine, low), high)
    mine, low, high = jnp.exp2(mine - peak), jnp.exp2(low - peak), jnp.exp2(high - peak)
    total = 1.0 / (mine + low + high)
    mine, low, high = mine * total, low * total, high * total
    for h in range(heads):
        cols = slice(h * HD, (h + 1) * HD)
        gate = gate_ref[pl.ds(head * heads + h, 1), :]
        mixed = o_ref[:, cols] * mine[:, h : h + 1]
        mixed = mixed + low_ref[:, cols].astype(jnp.float32) * low[:, h : h + 1]
        mixed = mixed + high_ref[:, cols].astype(jnp.float32) * high[:, h : h + 1]
        out_ref[:, cols] = (mixed * gate).astype(jnp.bfloat16)


def attention_cost(tiles, rows, cached, width):
    pairs = tiles * TILE * (rows + cached)
    return pl.CostEstimate(
        flops=4 * pairs * width, bytes_accessed=4 * (rows + cached) * width, transcendentals=pairs * (width // HD)
    )


def local(queries, keys, values, cache_keys, cache_values, pattern, reached, gate):
    split = lax.axis_size("head")
    count = lax.axis_size("ctx")
    part, full = queries.shape
    width = full // split
    rows = part * split
    cached = cache_keys.shape[0]
    own = rows // TILE
    up = [(i, i + 1) for i in range(count - 1)]
    down = [(i + 1, i) for i in range(count - 1)]

    def blocks(x):
        return jnp.transpose(x.reshape(part, split, width), (1, 0, 2))

    q = lax.all_to_all(blocks(queries), "head", split_axis=0, concat_axis=0, tiled=True).reshape(rows, width)
    kv = jnp.stack([blocks(keys), blocks(values)], axis=1)
    q, kv = lax.optimization_barrier((q, kv))
    from_below = lax.ppermute(q, "ctx", up)
    from_above = lax.ppermute(q, "ctx", down)
    kv = lax.all_to_all(kv, "head", split_axis=0, concat_axis=0, tiled=True)

    keys_seen = rows + cached
    partial = jax.ShapeDtypeStruct((rows, width + HD), jnp.bfloat16)
    to_below, to_above = pl.pallas_call(
        far_kernel,
        out_shape=(partial, partial),
        in_specs=[smem(), smem()] + [vmem()] * 5,
        out_specs=(vmem(), vmem()),
        scratch_shapes=[pltpu.VMEM((2 * own, 8, keys_seen), jnp.float32)],
        cost_estimate=attention_cost(2 * own, rows, cached, width),
        compiler_params=pltpu.CompilerParams(vmem_limit_bytes=LIMIT),
        name="far",
    )(pattern, reached, from_below, from_above, kv, cache_keys, cache_values)
    got_high = lax.ppermute(to_below, "ctx", down)
    got_low = lax.ppermute(to_above, "ctx", up)
    mine, stats = pl.pallas_call(
        own_kernel,
        out_shape=(
            jax.ShapeDtypeStruct((rows, width), jnp.float32),
            jax.ShapeDtypeStruct((rows, HD), jnp.float32),
        ),
        in_specs=[smem(), smem()] + [vmem()] * 4,
        out_specs=(vmem(), vmem()),
        scratch_shapes=[pltpu.VMEM((own, 8, keys_seen), jnp.float32)],
        cost_estimate=attention_cost(own, rows, cached, width),
        compiler_params=pltpu.CompilerParams(vmem_limit_bytes=LIMIT),
        name="own",
    )(pattern, reached, q, kv, cache_keys, cache_values)
    out = pl.pallas_call(
        functools.partial(mix_kernel, count),
        out_shape=jax.ShapeDtypeStruct((rows, width), jnp.bfloat16),
        in_specs=[vmem()] * 5,
        out_specs=vmem(),
        compiler_params=pltpu.CompilerParams(vmem_limit_bytes=LIMIT),
        name="mix",
    )(mine, stats, got_low, got_high, gate.reshape(full // HD, HD))
    out = lax.all_to_all(out.reshape(split, part, width), "head", split_axis=0, concat_axis=0, tiled=True)
    return jnp.transpose(out, (1, 0, 2)).reshape(part, full)


def solution(mesh):
    tokens = P(("ctx", "head"), None)
    cached = P("ctx", "head")
    return jax.shard_map(
        local,
        mesh=mesh,
        in_specs=(tokens, tokens, tokens, cached, cached, P(), P(), P()),
        out_specs=tokens,
        check_vma=False,
    )
```

time: 330 us -> 159 us (0.48)
  the two profiles are of different devices: /device:TPU:256 before, /device:TPU:30 now
where the time goes in v1:
time: 159 us
  waiting for transfers between devices  72.6 us (46%)
  blocking collectives  37.7 us (24%)
  starting transfers between devices  28.9 us (18%)
  Pallas kernels  15.6 us (10%)
  local copies, waits for them, and re-layouts  2.77 us (2%)
    all_to_all x1, blocking collectives, local(): lax.all_to_all(out.reshape(split, part, width), 'head', split_axis=0, con...  37.7 us
    ppermute x1, waiting for transfers between devices, local(): got_high = lax.ppermute(to_below, 'ctx', down)  27.2 us
    ppermute x1, waiting for transfers between devices, local(): from_above = lax.ppermute(q, 'ctx', down)  21 us
    ppermute x1, waiting for transfers between devices, local(): from_below = lax.ppermute(q, 'ctx', up)  11.5 us
    all_to_all x1, waiting for transfers between devices, local(): lax.all_to_all(blocks(queries), 'head', split_axis=0, concat_axis=0, tile...  11.4 us
    pallas_call x1, Pallas kernels, local(): pl.pallas_call(far_kernel, out_shape=(partial, partial), in_specs=[smem()...  9.22 us
    ppermute x1, starting transfers between devices, local(): from_below = lax.ppermute(q, 'ctx', up)  8.67 us
    ppermute x1, starting transfers between devices, local(): got_low = lax.ppermute(to_above, 'ctx', up)  6.65 us
  transfers between devices with their start and end apart: 6, of which 5 were waited for; matrix products, arithmetic and copies ran while one was open for 1% of the time, Pallas kernels for 3%

profile of v1, /device:TPU:30, one launch (start us, length us, event | category | flops | bytes accessed | tf_op | source)
XLA Modules:
  0.0 158.7 jit_solution(656884262779046483)
XLA Ops:
  0.0 1.8 %copy.26 = bf16[4,8,8,768]{3,2,0,1:T(8,128)(2,1)} copy(bf16[4,8,8,768]{3,2,1,0:T(8,128)(2,1)} %bitcast.33) | data formatting | bytes 786432 | tf_op jit(solution)/shard_map/reshape | solution.py:178
  1.8 0.0 copy-start.4
  1.8 0.0 copy-start.5
  1.8 6.0 %all-to-all-start = ((bf16[8,32,768]{2,1,0:T(8,128)(2,1)}), bf16[8,32,768]{2,1,0:T(8,128)(2,1)S(1)}, u32[]{:S(2)}, u32[]{:S(2)}) async-start(bf16[8,32,768]{2,1,0:T(8,128)(2,1)} %bitcast.26), calls=%async_computation | async-start | bytes 786432 | tf_op jit(solution)/shard_map/all_to_all | solution.py:180
  7.8 0.0 copy-done.4
  7.8 0.0 copy-done.5
  7.8 0.1 bitcast_bitcast_fusion
  7.9 0.0 copy-start.6
  7.9 1.0 pad_maximum_fusion
  8.9 11.4 %all-to-all-done = bf16[8,32,768]{2,1,0:T(8,128)(2,1)S(1)} async-done(((bf16[8,32,768]{2,1,0:T(8,128)(2,1)}), bf16[8,32,768]{2,1,0:T(8,128)(2,1)S(1)}, u32[]{:S(2)}, u32[]{:S(2)}) %all-to-all-start) | async-done | bytes 393248 | tf_op jit(solution)/shard_map/all_to_all | solution.py:180
  20.3 0.0 copy-start
  20.3 0.0 copy-start.1
  20.3 3.7 %all-to-all-start.1 = ((bf16[8,2,32,768]{3,2,1,0:T(8,128)(2,1)}), bf16[8,2,32,768]{3,2,1,0:T(8,128)(2,1)S(1)}, u32[]{:S(2)}, u32[]{:S(2)}) async-start(bf16[8,2,32,768]{3,2,1,0:T(8,128)(2,1)} %pad_maximum_fusion), calls=%async_computation.1 | async-start | bytes 1572864 | tf_op jit(solution)/shard_map/all_to_all | solution.py:185
  24.0 0.0 copy-start.3
  24.0 8.7 %collective-permute-start = (bf16[256,768]{1,0:T(8,128)(2,1)S(1)}, bf16[256,768]{1,0:T(8,128)(2,1)S(1)}, u32[]{:S(2)}, u32[]{:S(2)}) collective-permute-start(bf16[256,768]{1,0:T(8,128)(2,1)S(1)} %bitcast.27), channel_id=1, source_target_pairs={{0,8},{8,16},{16,24},{24,32},{32,40},{40,48},{48,56},{56,64},{64,7... | collective-permute-start | bytes 1179656 | tf_op jit(solution)/shard_map/ppermute | solution.py:183
  32.7 1.9 %collective-permute-start.1 = (bf16[256,768]{1,0:T(8,128)(2,1)S(1)}, bf16[256,768]{1,0:T(8,128)(2,1)}, u32[]{:S(2)}, u32[]{:S(2)}) collective-permute-start(bf16[256,768]{1,0:T(8,128)(2,1)S(1)} %bitcast.28), channel_id=1, source_target_pairs={{8,0},{16,8},{24,16},{32,24},{40,32},{48,40},{56,48},{64,56},{72,6... | collective-permute-start | bytes 1179656 | tf_op jit(solution)/shard_map/ppermute | solution.py:184
  34.6 0.0 copy-done.6
  34.6 0.1 copy.16.pattern_ref
  34.8 11.5 %collective-permute-done.below_ref = bf16[256,768]{1,0:T(8,128)(2,1)S(1)} collective-permute-done((bf16[256,768]{1,0:T(8,128)(2,1)S(1)}, bf16[256,768]{1,0:T(8,128)(2,1)S(1)}, u32[]{:S(2)}, u32[]{:S(2)}) %collective-permute-start) | collective-permute-done | bytes 393248 | tf_op jit(solution)/shard_map/ppermute | solution.py:183
  46.2 21.0 %collective-permute-done.1.above_ref = bf16[256,768]{1,0:T(8,128)(2,1)} collective-permute-done((bf16[256,768]{1,0:T(8,128)(2,1)S(1)}, bf16[256,768]{1,0:T(8,128)(2,1)}, u32[]{:S(2)}, u32[]{:S(2)}) %collective-permute-start.1) | collective-permute-done | bytes 393248 | tf_op jit(solution)/shard_map/ppermute | solution.py:184
  67.2 0.0 all-to-all-done.1.kv_ref
  67.2 0.0 copy-done
  67.2 0.0 copy-done.1
  67.2 0.0 copy-done.3
  67.2 9.2 %far.1 = (bf16[256,896]{1,0:T(8,128)(2,1)S(1)}, bf16[256,896]{1,0:T(8,128)(2,1)S(1)}) custom-call(s32[128,4]{1,0:T(8,128)S(1)} %copy.16.pattern_ref, s32[128]{0:T(128)S(1)} %copy-done.3, bf16[256,768]{1,0:T(8,128)(2,1)S(1)} %collective-permute-done.below_ref, bf16[256,768]{1,0:T(8,128)(2,1)} %collective-permute-done.1.above_ref, ...), custom_call_target="tpu_custom_call" | custom-call | flops 1207959552 | bytes 2359296 | tf_op jit(solution)/shard_map/far/pallas_call | solution.py:189
  76.5 6.6 %collective-permute-start.2 = (bf16[256,896]{1,0:T(8,128)(2,1)S(1)}, bf16[256,896]{1,0:T(8,128)(2,1)S(1)}, u32[]{:S(2)}, u32[]{:S(2)}) collective-permute-start(bf16[256,896]{1,0:T(8,128)(2,1)S(1)} %get-tuple-element.15), channel_id=1, source_target_pairs={{0,8},{8,16},{16,24},{24,32},{32,40},{40,48},{48,56},{56,64},{64,7... | collective-permute-start | bytes 1376264 | tf_op jit(solution)/shard_map/ppermute | solution.py:200
  83.1 0.0 copy-start.2
  83.1 1.9 %collective-permute-start.3 = (bf16[256,896]{1,0:T(8,128)(2,1)S(1)}, bf16[256,896]{1,0:T(8,128)(2,1)S(1)}, u32[]{:S(2)}, u32[]{:S(2)}) collective-permute-start(bf16[256,896]{1,0:T(8,128)(2,1)S(1)} %get-tuple-element.16), channel_id=1, source_target_pairs={{8,0},{16,8},{24,16},{32,24},{40,32},{48,40},{56,48},{64,56},{72,6... | collective-permute-start | bytes 1376264 | tf_op jit(solution)/shard_map/ppermute | solution.py:199
  85.1 5.5 %own.1 = (f32[256,768]{1,0:T(8,128)S(1)}, f32[256,128]{1,0:T(8,128)S(1)}) custom-call(s32[128,4]{1,0:T(8,128)S(1)} %copy.16.pattern_ref, s32[128]{0:T(128)S(1)} %copy-done.3, bf16[256,768]{1,0:T(8,128)(2,1)S(1)} %bitcast.29, bf16[8,2,32,768]{3,2,1,0:T(8,128)(2,1)S(1)} %all-to-all-done.1.kv_ref, bf16[512,768]{1,0:T(8,128)(2,1)S(1)} %copy-done, ...), custom_call_target="tpu_custom_call" | custom-call | flops 603979776 | bytes 2359296 | tf_op jit(solution)/shard_map/own/pallas_call | solution.py:201
  90.5 1.5 collective-permute-done.2.low_ref
  92.0 27.2 %collective-permute-done.3.high_ref = bf16[256,896]{1,0:T(8,128)(2,1)S(1)} collective-permute-done((bf16[256,896]{1,0:T(8,128)(2,1)S(1)}, bf16[256,896]{1,0:T(8,128)(2,1)S(1)}, u32[]{:S(2)}, u32[]{:S(2)}) %collective-permute-start.3) | collective-permute-done | bytes 458784 | tf_op jit(solution)/shard_map/ppermute | solution.py:199
  119.3 0.0 copy-done.2
  119.3 0.9 mix.1
  120.2 37.7 %all_to_all.15 = bf16[8,32,768]{2,1,0:T(8,128)(2,1)S(1)} all-to-all(bf16[8,32,768]{2,1,0:T(8,128)(2,1)S(1)} %bitcast.30), channel_id=1, replica_groups=mesh['ctx'=64,'head'=8] {'head'}, dimensions={0} | all-to-all | bytes 786432 | tf_op jit(solution)/shard_map/all_to_all | solution.py:222
  157.9 0.8 copy.22
Async XLA Ops:
  1.8 6.0 %copy-start.4 = (bf16[32,6144]{1,0:T(8,128)(2,1)S(1)}, bf16[32,6144]{1,0:T(8,128)(2,1)}, u32[]{:S(2)}) copy-start(bf16[32,6144]{1,0:T(8,128)(2,1)} %param.10) | copy-start | bytes 1179652
  1.8 6.0 %copy-start.5 = (bf16[32,6144]{1,0:T(8,128)(2,1)S(1)}, bf16[32,6144]{1,0:T(8,128)(2,1)}, u32[]{:S(2)}) copy-start(bf16[32,6144]{1,0:T(8,128)(2,1)} %param.9) | copy-start | bytes 1179652
  1.8 18.6 %all-to-all-start = ((bf16[8,32,768]{2,1,0:T(8,128)(2,1)}), bf16[8,32,768]{2,1,0:T(8,128)(2,1)S(1)}, u32[]{:S(2)}, u32[]{:S(2)}) async-start(bf16[8,32,768]{2,1,0:T(8,128)(2,1)} %bitcast.26), calls=%async_computation | async-start | bytes 786432 | tf_op jit(solution)/shard_map/all_to_all | solution.py:180
  7.9 26.7 %copy-start.6 = (s32[128,4]{0,1:T(4,128)S(1)}, s32[128,4]{0,1:T(4,128)}, u32[]{:S(2)}) copy-start(s32[128,4]{0,1:T(4,128)} %param.13) | copy-start | bytes 6148
  20.3 46.9 %copy-start = (bf16[512,768]{1,0:T(8,128)(2,1)S(1)}, bf16[512,768]{1,0:T(8,128)(2,1)}, u32[]{:S(2)}) copy-start(bf16[512,768]{1,0:T(8,128)(2,1)} %ck_ref.3) | copy-start | bytes 2359300
  20.3 46.9 %copy-start.1 = (bf16[512,768]{1,0:T(8,128)(2,1)S(1)}, bf16[512,768]{1,0:T(8,128)(2,1)}, u32[]{:S(2)}) copy-start(bf16[512,768]{1,0:T(8,128)(2,1)} %cv_ref.3) | copy-start | bytes 2359300
  20.3 46.9 %all-to-all-start.1 = ((bf16[8,2,32,768]{3,2,1,0:T(8,128)(2,1)}), bf16[8,2,32,768]{3,2,1,0:T(8,128)(2,1)S(1)}, u32[]{:S(2)}, u32[]{:S(2)}) async-start(bf16[8,2,32,768]{3,2,1,0:T(8,128)(2,1)} %pad_maximum_fusion), calls=%async_computation.1 | async-start | bytes 1572864 | tf_op jit(solution)/shard_map/all_to_all | solution.py:185
  24.0 43.2 %copy-start.3 = (s32[128]{0:T(128)S(1)}, s32[128]{0:T(128)}, u32[]{:S(2)}) copy-start(s32[128]{0:T(128)} %reached_ref.3) | copy-start | bytes 1540
  24.0 22.2 %collective-permute-start = (bf16[256,768]{1,0:T(8,128)(2,1)S(1)}, bf16[256,768]{1,0:T(8,128)(2,1)S(1)}, u32[]{:S(2)}, u32[]{:S(2)}) collective-permute-start(bf16[256,768]{1,0:T(8,128)(2,1)S(1)} %bitcast.27), channel_id=1, source_target_pairs={{0,8},{8,16},{16,24},{24,32},{32,40},{40,48},{48,56},{56,64},{64,7... | collective-permute-start | bytes 1179656 | tf_op jit(solution)/shard_map/ppermute | solution.py:183
  32.7 34.5 %collective-permute-start.1 = (bf16[256,768]{1,0:T(8,128)(2,1)S(1)}, bf16[256,768]{1,0:T(8,128)(2,1)}, u32[]{:S(2)}, u32[]{:S(2)}) collective-permute-start(bf16[256,768]{1,0:T(8,128)(2,1)S(1)} %bitcast.28), channel_id=1, source_target_pairs={{8,0},{16,8},{24,16},{32,24},{40,32},{48,40},{56,48},{64,56},{72,6... | collective-permute-start | bytes 1179656 | tf_op jit(solution)/shard_map/ppermute | solution.py:184
  76.5 15.5 %collective-permute-start.2 = (bf16[256,896]{1,0:T(8,128)(2,1)S(1)}, bf16[256,896]{1,0:T(8,128)(2,1)S(1)}, u32[]{:S(2)}, u32[]{:S(2)}) collective-permute-start(bf16[256,896]{1,0:T(8,128)(2,1)S(1)} %get-tuple-element.15), channel_id=1, source_target_pairs={{0,8},{8,16},{16,24},{24,32},{32,40},{40,48},{48,56},{56,64},{64,7... | collective-permute-start | bytes 1376264 | tf_op jit(solution)/shard_map/ppermute | solution.py:200
  83.1 36.1 %copy-start.2 = (f32[6144]{0:T(1024)S(1)}, f32[6144]{0:T(1024)}, u32[]{:S(2)}) copy-start(f32[6144]{0:T(1024)} %param.15) | copy-start | bytes 73732
  83.1 36.1 %collective-permute-start.3 = (bf16[256,896]{1,0:T(8,128)(2,1)S(1)}, bf16[256,896]{1,0:T(8,128)(2,1)S(1)}, u32[]{:S(2)}, u32[]{:S(2)}) collective-permute-start(bf16[256,896]{1,0:T(8,128)(2,1)S(1)} %get-tuple-element.16), channel_id=1, source_target_pairs={{8,0},{16,8},{24,16},{32,24},{40,32},{48,40},{56,48},{64,56},{72,6... | collective-permute-start | bytes 1376264 | tf_op jit(solution)/shard_map/ppermute | solution.py:199

commit v2 on v1

--- a/solution.py
+++ b/solution.py
@@ -8,11 +8,14 @@
 from jax.experimental.pallas import tpu as pltpu
 from jax.sharding import PartitionSpec as P
 
+
 HD = 128
 TILE = 128
 REACH = 4
 NEGATIVE = -1e30
 LIMIT = 24 << 20
+PLANE = 16
+SWAPPED = 112
 LOG2E = math.log2(math.e)
 NT = (((1,), (1,)), ((), ()))
 
@@ -72,19 +75,21 @@
 
 
 def pieces(lse):
-    high = lse.astype(jnp.bfloat16).astype(jnp.float32)
-    rest = lse - high
-    middle = rest.astype(jnp.bfloat16).astype(jnp.float32)
-    low = rest - middle
-    return (high + pltpu.roll(middle, 32, 1) + pltpu.roll(low, 64, 1)).astype(jnp.bfloat16)
-
-
-def whole(block):
-    block = block.astype(jnp.float32)
-    return block + pltpu.roll(block, 96, 1) + pltpu.roll(block, 64, 1)
-
-
-def attend_all(q_ref, kv_ref, ck_ref, cv_ref, bias_ref, first_row, put):
+    lse = jnp.transpose(lse)[:16]
+    high = lse.astype(jnp.bfloat16)
+    rest = lse - high.astype(jnp.float32)
+    middle = rest.astype(jnp.bfloat16)
+    low = (rest - middle.astype(jnp.float32)).astype(jnp.bfloat16)
+    return high, middle, low
+
+
+def whole(rows):
+    rows = rows.astype(jnp.float32)
+    lse = rows[:, :TILE] + rows[:, TILE : 2 * TILE] + rows[:, 2 * TILE :]
+    return jnp.transpose(jnp.concatenate([lse] * (HD // 16), axis=0))
+
+
+def attend_all(load, kv_ref, ck_ref, cv_ref, bias_ref, first_row, put):
     parts, _, part, width = kv_ref.shape
     rows = parts * part
     lane = lax.broadcasted_iota(jnp.int32, (TILE, HD), 1)
@@ -93,7 +98,7 @@
         stats = jnp.zeros((TILE, HD), jnp.float32)
         for h in range(width // HD):
             cols = slice(h * HD, (h + 1) * HD)
-            q = q_ref[t * TILE : (t + 1) * TILE, cols]
+            q = load(t, cols)
             k = kv_ref[:, 0, :, cols].reshape(rows, HD)
             v = kv_ref[:, 1, :, cols].reshape(rows, HD)
             out, lse = attend(q, k, v, ck_ref[:, cols], cv_ref[:, cols], bias)
@@ -103,22 +108,54 @@
 
 
 def far_kernel(
-    pattern_ref, reached_ref, below_ref, above_ref, kv_ref, ck_ref, cv_ref, to_below_ref, to_above_ref, bias_ref
+    pattern_ref,
+    reached_ref,
+    below_ref,
+    above_ref,
+    direct_ref,
+    swapped_ref,
+    kv_ref,
+    ck_ref,
+    cv_ref,
+    to_below_ref,
+    to_above_ref,
+    to_direct_ref,
+    to_swapped_ref,
+    bias_ref,
 ):
     own = kv_ref.shape[0] * kv_ref.shape[2] // TILE
     rel = tuple(range(-own, 0)) + tuple(range(own, 2 * own))
     fill_bias(bias_ref, pattern_ref, reached_ref, rel, own, ck_ref.shape[0] // TILE)
-    width = kv_ref.shape[3]
-    for side, (q_ref, o_ref) in enumerate(((below_ref, to_below_ref), (above_ref, to_above_ref))):
+    rows = own * TILE
+    near = direct_ref.shape[0]
+    at = lax.rem(lax.axis_index("ctx"), PLANE)
+    sides = ((below_ref, to_below_ref, at == 0), (above_ref, to_above_ref, at == PLANE - 1))
+    for side, (q_ref, o_ref, jumps) in enumerate(sides):
+
+        def load(t, cols, q_ref=q_ref, jumps=jumps):
+            low, high = t * TILE, (t + 1) * TILE
+            if high <= near:
+                jumped = direct_ref[low:high, cols]
+            elif low >= near:
+                jumped = swapped_ref[low - near : high - near, cols]
+            else:
+                jumped = jnp.concatenate([direct_ref[low:, cols], swapped_ref[: high - near, cols]], axis=0)
+            return jnp.where(jumps, jumped, q_ref[low:high, cols])
 
         def put(t, cols, value, o_ref=o_ref):
-            rows = slice(t * TILE, (t + 1) * TILE)
             if cols is None:
-                o_ref[rows, width:] = pieces(value)
+                for i, piece in enumerate(pieces(value)):
+                    o_ref[rows:, (3 * t + i) * TILE : (3 * t + i + 1) * TILE] = piece
             else:
-                o_ref[rows, cols] = value.astype(jnp.bfloat16)
-
-        attend_all(q_ref, kv_ref, ck_ref, cv_ref, bias_ref, side * own, put)
+                o_ref[t * TILE : (t + 1) * TILE, cols] = value.astype(jnp.bfloat16)
+
+        attend_all(load, kv_ref, ck_ref, cv_ref, bias_ref, side * own, put)
+
+        @pl.when(jumps)
+        def _(o_ref=o_ref):
+            direct = to_direct_ref.shape[0]
+            to_direct_ref[...] = o_ref[:direct]
+            to_swapped_ref[...] = o_ref[direct:]
 
 
 def own_kernel(pattern_ref, reached_ref, q_ref, kv_ref, ck_ref, cv_ref, o_ref, stats_ref, bias_ref):
@@ -132,28 +169,48 @@
         else:
             o_ref[rows, cols] = value
 
-    attend_all(q_ref, kv_ref, ck_ref, cv_ref, bias_ref, 0, put)
-
-
-def mix_kernel(count, o_ref, stats_ref, low_ref, high_ref, gate_ref, out_ref):
+    def load(t, cols):
+        return q_ref[t * TILE : (t + 1) * TILE, cols]
+
+    attend_all(load, kv_ref, ck_ref, cv_ref, bias_ref, 0, put)
+
+
+def mix_kernel(count, o_ref, stats_ref, low_ref, high_ref, direct_ref, swapped_ref, gate_ref, out_ref):
     ctx = lax.axis_index("ctx")
+    at = lax.rem(ctx, PLANE)
+    first, last = at == 0, at == PLANE - 1
     head = lax.axis_index("head")
     rows, width = o_ref.shape
     heads = width // HD
-    mine = stats_ref[...]
-    low = jnp.where(ctx > 0, whole(low_ref[:, width:]), NEGATIVE)
-    high = jnp.where(ctx < count - 1, whole(high_ref[:, width:]), NEGATIVE)
-    peak = jnp.maximum(jnp.maximum(mine, low), high)
-    mine, low, high = jnp.exp2(mine - peak), jnp.exp2(low - peak), jnp.exp2(high - peak)
-    total = 1.0 / (mine + low + high)
-    mine, low, high = mine * total, low * total, high * total
-    for h in range(heads):
-        cols = slice(h * HD, (h + 1) * HD)
-        gate = gate_ref[pl.ds(head * heads + h, 1), :]
-        mixed = o_ref[:, cols] * mine[:, h : h + 1]
-        mixed = mixed + low_ref[:, cols].astype(jnp.float32) * low[:, h : h + 1]
-        mixed = mixed + high_ref[:, cols].astype(jnp.float32) * high[:, h : h + 1]
-        out_ref[:, cols] = (mixed * gate).astype(jnp.bfloat16)
+    near = direct_ref.shape[0]
+    for t in range(rows // TILE):
+        here = slice(t * TILE, (t + 1) * TILE)
+        stat = slice(rows - near, None), slice(3 * t * TILE, 3 * (t + 1) * TILE)
+        jumped = swapped_ref[stat]
+        stat = slice(rows, None), stat[1]
+        low = whole(jnp.where(first, jumped, low_ref[stat]))
+        high = whole(jnp.where(last, jumped, high_ref[stat]))
+        low = jnp.where(ctx > 0, low, NEGATIVE)
+        high = jnp.where(ctx < count - 1, high, NEGATIVE)
+        mine = stats_ref[here, :]
+        peak = jnp.maximum(jnp.maximum(mine, low), high)
+        mine, low, high = jnp.exp2(mine - peak), jnp.exp2(low - peak), jnp.exp2(high - peak)
+        total = 1.0 / (mine + low + high)
+        mine, low, high = mine * total, low * total, high * total
+        for h in range(heads):
+            cols = slice(h * HD, (h + 1) * HD)
+            start, stop = t * TILE, (t + 1) * TILE
+            if stop <= near:
+                jumped = direct_ref[start:stop, cols]
+            elif start >= near:
+                jumped = swapped_ref[start - near : stop - near, cols]
+            else:
+                jumped = jnp.concatenate([direct_ref[start:, cols], swapped_ref[: stop - near, cols]], axis=0)
+            gate = gate_ref[pl.ds(head * heads + h, 1), :]
+            mixed = o_ref[here, cols] * mine[:, h : h + 1]
+            mixed = mixed + jnp.where(first, jumped, low_ref[here, cols]).astype(jnp.float32) * low[:, h : h + 1]
+            mixed = mixed + jnp.where(last, jumped, high_ref[here, cols]).astype(jnp.float32) * high[:, h : h + 1]
+            out_ref[here, cols] = (mixed * gate).astype(jnp.bfloat16)
 
 
 def attention_cost(tiles, rows, cached, width):
@@ -171,8 +228,17 @@
     rows = part * split
     cached = cache_keys.shape[0]
     own = rows // TILE
-    up = [(i, i + 1) for i in range(count - 1)]
-    down = [(i + 1, i) for i in range(count - 1)]
+    firsts = range(0, count, PLANE)
+    jumps = [(first - 1, first) for first in firsts if first]
+    inside = [(i, i + 1) for i in range(count - 1) if (i + 1) % PLANE]
+    up = inside
+    down = [(b, a) for a, b in inside]
+    straight = jumps + [(b, a) for a, b in jumps]
+    swap = [(a, a + 1 - PLANE) for a, _ in jumps] + [(b, b - 1 + PLANE) for _, b in jumps]
+    onward = [(a + 1 - PLANE, b) for a, b in jumps] + [(b - 1 + PLANE, a) for a, b in jumps]
+
+    def shift(x, pairs):
+        return lax.ppermute(x, "ctx", pairs)
 
     def blocks(x):
         return jnp.transpose(x.reshape(part, split, width), (1, 0, 2))
@@ -180,24 +246,31 @@
     q = lax.all_to_all(blocks(queries), "head", split_axis=0, concat_axis=0, tiled=True).reshape(rows, width)
     kv = jnp.stack([blocks(keys), blocks(values)], axis=1)
     q, kv = lax.optimization_barrier((q, kv))
-    from_below = lax.ppermute(q, "ctx", up)
-    from_above = lax.ppermute(q, "ctx", down)
+    swapped = shift(q[rows - SWAPPED :], swap)
+    direct = shift(q[: rows - SWAPPED], straight)
+    swapped = shift(swapped, onward)
+    from_below = shift(q, up)
+    from_above = shift(q, down)
     kv = lax.all_to_all(kv, "head", split_axis=0, concat_axis=0, tiled=True)
 
     keys_seen = rows + cached
-    partial = jax.ShapeDtypeStruct((rows, width + HD), jnp.bfloat16)
-    to_below, to_above = pl.pallas_call(
+    partial = rows + 16
+    shapes = [partial, partial, partial - SWAPPED, SWAPPED]
+    to_below, to_above, to_direct, to_swapped = pl.pallas_call(
         far_kernel,
-        out_shape=(partial, partial),
-        in_specs=[smem(), smem()] + [vmem()] * 5,
-        out_specs=(vmem(), vmem()),
+        out_shape=tuple(jax.ShapeDtypeStruct((n, width), jnp.bfloat16) for n in shapes),
+        in_specs=[smem(), smem()] + [vmem()] * 7,
+        out_specs=(vmem(),) * 4,
         scratch_shapes=[pltpu.VMEM((2 * own, 8, keys_seen), jnp.float32)],
         cost_estimate=attention_cost(2 * own, rows, cached, width),
         compiler_params=pltpu.CompilerParams(vmem_limit_bytes=LIMIT),
         name="far",
-    )(pattern, reached, from_below, from_above, kv, cache_keys, cache_values)
-    got_high = lax.ppermute(to_below, "ctx", down)
-    got_low = lax.ppermute(to_above, "ctx", up)
+    )(pattern, reached, from_below, from_above, direct, swapped, kv, cache_keys, cache_values)
+    swapped = shift(to_swapped, swap)
+    direct = shift(to_direct, straight)
+    got_high = shift(to_below, down)
+    got_low = shift(to_above, up)
+    swapped = shift(swapped, onward)
     mine, stats = pl.pallas_call(
         own_kernel,
         out_shape=(
@@ -214,11 +287,11 @@
     out = pl.pallas_call(
         functools.partial(mix_kernel, count),
         out_shape=jax.ShapeDtypeStruct((rows, width), jnp.bfloat16),
-        in_specs=[vmem()] * 5,
+        in_specs=[vmem()] * 7,
         out_specs=vmem(),
         compiler_params=pltpu.CompilerParams(vmem_limit_bytes=LIMIT),
         name="mix",
-    )(mine, stats, got_low, got_high, gate.reshape(full // HD, HD))
+    )(mine, stats, got_low, got_high, direct, swapped, gate.reshape(full // HD, HD))
     out = lax.all_to_all(out.reshape(split, part, width), "head", split_axis=0, concat_axis=0, tiled=True)
     return jnp.transpose(out, (1, 0, 2)).reshape(part, full)
 

time: 159 us -> 134 us (0.84)
  the two profiles are of different devices: /device:TPU:30 before, /device:TPU:128 now
where the time goes in v2:
time: 134 us
  starting transfers between devices  65.9 us (49%)
  blocking collectives  24.4 us (18%)
  waiting for transfers between devices  23 us (17%)
  Pallas kernels  15.7 us (12%)
  local copies, waits for them, and re-layouts  3.48 us (3%)
    ppermute x10, starting transfers between devices, shift(): return lax.ppermute(x, 'ctx', pairs)  56.2 us
    all_to_all x1, blocking collectives, local(): lax.all_to_all(out.reshape(split, part, width), 'head', split_axis=0, con...  24.4 us
    ppermute x10, waiting for transfers between devices, shift(): return lax.ppermute(x, 'ctx', pairs)  11.5 us
    all_to_all x1, waiting for transfers between devices, local(): lax.all_to_all(blocks(queries), 'head', split_axis=0, concat_axis=0, tile...  11.5 us
    pallas_call x1, Pallas kernels, local(): pl.pallas_call(far_kernel, out_shape=tuple((jax.ShapeDtypeStruct((n, widt...  9.38 us
    all_to_all x1, starting transfers between devices, local(): lax.all_to_all(blocks(queries), 'head', split_axis=0, concat_axis=0, tile...  6.03 us
    pallas_call x1, Pallas kernels, local(): pl.pallas_call(own_kernel, out_shape=(jax.ShapeDtypeStruct((rows, width),...  5.5 us
    all_to_all x1, starting transfers between devices, local(): kv = lax.all_to_all(kv, 'head', split_axis=0, concat_axis=0, tiled=True)  3.68 us
  transfers between devices with their start and end apart: 12, of which 5 were waited for; matrix products, arithmetic and copies ran while one was open for 1% of the time, Pallas kernels for 4%

profile of v2, /device:TPU:128, one launch (start us, length us, event | category | flops | bytes accessed | tf_op | source)
XLA Modules:
  0.0 133.7 jit_solution(16972238972819539990)
XLA Ops:
  0.0 1.8 %copy.26 = bf16[4,8,8,768]{3,2,0,1:T(8,128)(2,1)} copy(bf16[4,8,8,768]{3,2,1,0:T(8,128)(2,1)} %bitcast.35) | data formatting | bytes 786432 | tf_op jit(solution)/shard_map/reshape | solution.py:244
  1.8 0.0 copy-start.4
  1.8 0.0 copy-start.5
  1.8 6.0 %all-to-all-start = ((bf16[8,32,768]{2,1,0:T(8,128)(2,1)}), bf16[8,32,768]{2,1,0:T(8,128)(2,1)S(1)}, u32[]{:S(2)}, u32[]{:S(2)}) async-start(bf16[8,32,768]{2,1,0:T(8,128)(2,1)} %bitcast.26), calls=%async_computation | async-start | bytes 786432 | tf_op jit(solution)/shard_map/all_to_all | solution.py:246
  7.8 0.0 copy-done.4
  7.8 0.0 copy-done.5
  7.8 0.1 bitcast_bitcast_fusion
  7.9 1.0 pad_maximum_fusion
  8.9 11.5 %all-to-all-done = bf16[8,32,768]{2,1,0:T(8,128)(2,1)S(1)} async-done(((bf16[8,32,768]{2,1,0:T(8,128)(2,1)}), bf16[8,32,768]{2,1,0:T(8,128)(2,1)S(1)}, u32[]{:S(2)}, u32[]{:S(2)}) %all-to-all-start) | async-done | bytes 393248 | tf_op jit(solution)/shard_map/all_to_all | solution.py:246
  20.3 0.0 copy-start.6
  20.3 0.0 copy-start.1
  20.3 3.7 %all-to-all-start.1 = ((bf16[8,2,32,768]{3,2,1,0:T(8,128)(2,1)}), bf16[8,2,32,768]{3,2,1,0:T(8,128)(2,1)S(1)}, u32[]{:S(2)}, u32[]{:S(2)}) async-start(bf16[8,2,32,768]{3,2,1,0:T(8,128)(2,1)} %pad_maximum_fusion), calls=%async_computation.1 | async-start | bytes 1572864 | tf_op jit(solution)/shard_map/all_to_all | solution.py:254
  24.0 0.0 copy-start
  24.0 1.4 %collective-permute-start.1 = (bf16[256,768]{1,0:T(8,128)(2,1)S(1)}, bf16[256,768]{1,0:T(8,128)(2,1)S(1)}, u32[]{:S(2)}, u32[]{:S(2)}) collective-permute-start(bf16[256,768]{1,0:T(8,128)(2,1)S(1)} %bitcast.27), channel_id=1, source_target_pairs={{8,0},{16,8},{24,16},{32,24},{40,32},{48,40},{56,48},{64,56},{72,6... | collective-permute-start | bytes 1179656 | tf_op jit(solution)/shard_map/ppermute | solution.py:241
  25.5 5.3 %collective-permute-start = (bf16[256,768]{1,0:T(8,128)(2,1)S(1)}, bf16[256,768]{1,0:T(8,128)(2,1)}, u32[]{:S(2)}, u32[]{:S(2)}) collective-permute-start(bf16[256,768]{1,0:T(8,128)(2,1)S(1)} %bitcast.28), channel_id=1, source_target_pairs={{0,8},{8,16},{16,24},{24,32},{32,40},{40,48},{48,56},{56,64},{64,7... | collective-permute-start | bytes 1179656 | tf_op jit(solution)/shard_map/ppermute | solution.py:241
  30.8 4.5 %collective-permute-start.3 = (bf16[112,768]{1,0:T(8,128)(2,1)S(1)}, bf16[112,768]{1,0:T(8,128)(2,1)}, u32[]{:S(2)}, u32[]{:S(2)}) collective-permute-start(bf16[112,768]{1,0:T(8,128)(2,1)S(1)} %slice.7), channel_id=1, source_target_pairs={{120,0},{248,128},{376,256},{128,248},{256,376},{384,504},{121,1},... | collective-permute-start | bytes 516104 | tf_op jit(solution)/shard_map/ppermute | solution.py:241
  35.3 0.7 slice.6
  36.0 0.0 copy-start.3
  36.0 6.5 %collective-permute-start.2 = (bf16[144,768]{1,0:T(8,128)(2,1)}, bf16[144,768]{1,0:T(8,128)(2,1)S(1)}, u32[]{:S(2)}, u32[]{:S(2)}) collective-permute-start(bf16[144,768]{1,0:T(8,128)(2,1)} %slice.6), channel_id=1, source_target_pairs={{120,128},{248,256},{376,384},{128,120},{256,248},{384,376},{121,1... | collective-permute-start | bytes 663560 | tf_op jit(solution)/shard_map/ppermute | solution.py:241
  42.5 0.0 collective-permute-done.3
  42.5 6.3 %collective-permute-start.4 = (bf16[112,768]{1,0:T(8,128)(2,1)}, bf16[112,768]{1,0:T(8,128)(2,1)}, u32[]{:S(2)}, u32[]{:S(2)}) collective-permute-start(bf16[112,768]{1,0:T(8,128)(2,1)} %collective-permute-done.3), channel_id=1, source_target_pairs={{0,128},{128,256},{256,384},{248,120},{376,248},{504,376},{1,129},... | collective-permute-start | bytes 516104 | tf_op jit(solution)/shard_map/ppermute | solution.py:241
  48.8 0.0 copy-done.6
  48.8 0.1 copy.16.pattern_ref
  48.9 4.9 %collective-permute-done.2.direct_ref = bf16[144,768]{1,0:T(8,128)(2,1)S(1)} collective-permute-done((bf16[144,768]{1,0:T(8,128)(2,1)}, bf16[144,768]{1,0:T(8,128)(2,1)S(1)}, u32[]{:S(2)}, u32[]{:S(2)}) %collective-permute-start.2) | collective-permute-done | bytes 221216 | tf_op jit(solution)/shard_map/ppermute | solution.py:241
  53.8 0.6 collective-permute-done.4.swapped_ref
  54.4 0.0 collective-permute-done.1.above_ref
  54.4 0.0 collective-permute-done.below_ref
  54.5 0.0 all-to-all-done.1.kv_ref
  54.5 0.0 copy-done.1
  54.5 0.0 copy-done
  54.5 0.0 copy-done.3
  54.5 9.4 %far.1 = (bf16[272,768]{1,0:T(8,128)(2,1)S(1)}, bf16[272,768]{1,0:T(8,128)(2,1)S(1)}, bf16[160,768]{1,0:T(8,128)(2,1)S(1)}, bf16[112,768]{1,0:T(8,128)(2,1)S(1)}) custom-call(s32[128,4]{1,0:T(8,128)S(1)} %copy.16.pattern_ref, s32[128]{0:T(128)S(1)} %copy-done.3, bf16[256,768]{1,0:T(8,128)(2,1)} %collective-permute-done.below_ref, ...), custom_call_target="tpu_custom_call" | custom-call | flops 1207959552 | bytes 2359296 | tf_op jit(solution)/shard_map/far/pallas_call | solution.py:259
  63.9 1.3 collective-permute-start.5
  65.2 1.3 collective-permute-start.6
  66.5 21.2 %collective-permute-start.8 = (bf16[112,768]{1,0:T(8,128)(2,1)S(1)}, bf16[112,768]{1,0:T(8,128)(2,1)S(1)}, u32[]{:S(2)}, u32[]{:S(2)}) collective-permute-start(bf16[112,768]{1,0:T(8,128)(2,1)S(1)} %get-tuple-element.20), channel_id=1, source_target_pairs={{120,0},{248,128},{376,256},{128,248},{256,376},{384,504},{121,1},... | collective-permute-start | bytes 516104 | tf_op jit(solution)/shard_map/ppermute | solution.py:241
  87.7 0.0 copy-start.2
  87.7 2.0 %collective-permute-start.7 = (bf16[160,768]{1,0:T(8,128)(2,1)S(1)}, bf16[160,768]{1,0:T(8,128)(2,1)S(1)}, u32[]{:S(2)}, u32[]{:S(2)}) collective-permute-start(bf16[160,768]{1,0:T(8,128)(2,1)S(1)} %get-tuple-element.19), channel_id=1, source_target_pairs={{120,128},{248,256},{376,384},{128,120},{256,248},{384,376},{121,1... | collective-permute-start | bytes 737288 | tf_op jit(solution)/shard_map/ppermute | solution.py:241
  89.7 1.3 collective-permute-done.8
  91.1 6.4 %collective-permute-start.9 = (bf16[112,768]{1,0:T(8,128)(2,1)S(1)}, bf16[112,768]{1,0:T(8,128)(2,1)S(1)}, u32[]{:S(2)}, u32[]{:S(2)}) collective-permute-start(bf16[112,768]{1,0:T(8,128)(2,1)S(1)} %collective-permute-done.8), channel_id=1, source_target_pairs={{0,128},{128,256},{256,384},{248,120},{376,248},{504,376},{1,129},... | collective-permute-start | bytes 516104 | tf_op jit(solution)/shard_map/ppermute | solution.py:241
  97.5 5.5 %own.1 = (f32[256,768]{1,0:T(8,128)S(1)}, f32[256,128]{1,0:T(8,128)S(1)}) custom-call(s32[128,4]{1,0:T(8,128)S(1)} %copy.16.pattern_ref, s32[128]{0:T(128)S(1)} %copy-done.3, bf16[256,768]{1,0:T(8,128)(2,1)S(1)} %bitcast.31, bf16[8,2,32,768]{3,2,1,0:T(8,128)(2,1)S(1)} %all-to-all-done.1.kv_ref, bf16[512,768]{1,0:T(8,128)(2,1)S(1)} %copy-done, ...), custom_call_target="tpu_custom_call" | custom-call | flops 603979776 | bytes 2359296 | tf_op jit(solution)/shard_map/own/pallas_call | solution.py:274
  103.0 4.7 %collective-permute-done.7.direct_ref = bf16[160,768]{1,0:T(8,128)(2,1)S(1)} collective-permute-done((bf16[160,768]{1,0:T(8,128)(2,1)S(1)}, bf16[160,768]{1,0:T(8,128)(2,1)S(1)}, u32[]{:S(2)}, u32[]{:S(2)}) %collective-permute-start.7) | collective-permute-done | bytes 245792 | tf_op jit(solution)/shard_map/ppermute | solution.py:241
  107.6 0.0 collective-permute-done.9.swapped_ref
  107.7 0.0 collective-permute-done.5.low_ref
  107.7 0.0 collective-permute-done.6.high_ref
  107.7 0.0 copy-done.2
  107.7 0.8 mix.1
  108.5 24.4 %all_to_all.15 = bf16[8,32,768]{2,1,0:T(8,128)(2,1)S(1)} all-to-all(bf16[8,32,768]{2,1,0:T(8,128)(2,1)S(1)} %bitcast.32), channel_id=1, replica_groups=mesh['ctx'=64,'head'=8] {'head'}, dimensions={0} | all-to-all | bytes 786432 | tf_op jit(solution)/shard_map/all_to_all | solution.py:295
  133.0 0.8 copy.22
  (1 shorter events, 0.0 us)
Async XLA Ops:
  1.8 6.0 %copy-start.4 = (bf16[32,6144]{1,0:T(8,128)(2,1)S(1)}, bf16[32,6144]{1,0:T(8,128)(2,1)}, u32[]{:S(2)}) copy-start(bf16[32,6144]{1,0:T(8,128)(2,1)} %param.10) | copy-start | bytes 1179652
  1.8 6.0 %copy-start.5 = (bf16[32,6144]{1,0:T(8,128)(2,1)S(1)}, bf16[32,6144]{1,0:T(8,128)(2,1)}, u32[]{:S(2)}) copy-start(bf16[32,6144]{1,0:T(8,128)(2,1)} %param.9) | copy-start | bytes 1179652
  1.8 18.6 %all-to-all-start = ((bf16[8,32,768]{2,1,0:T(8,128)(2,1)}), bf16[8,32,768]{2,1,0:T(8,128)(2,1)S(1)}, u32[]{:S(2)}, u32[]{:S(2)}) async-start(bf16[8,32,768]{2,1,0:T(8,128)(2,1)} %bitcast.26), calls=%async_computation | async-start | bytes 786432 | tf_op jit(solution)/shard_map/all_to_all | solution.py:246
  20.3 28.5 %copy-start.6 = (s32[128,4]{0,1:T(4,128)S(1)}, s32[128,4]{0,1:T(4,128)}, u32[]{:S(2)}) copy-start(s32[128,4]{0,1:T(4,128)} %param.13) | copy-start | bytes 6148
  20.3 34.1 %copy-start.1 = (bf16[512,768]{1,0:T(8,128)(2,1)S(1)}, bf16[512,768]{1,0:T(8,128)(2,1)}, u32[]{:S(2)}) copy-start(bf16[512,768]{1,0:T(8,128)(2,1)} %cv_ref.3) | copy-start | bytes 2359300
  20.3 34.1 %all-to-all-start.1 = ((bf16[8,2,32,768]{3,2,1,0:T(8,128)(2,1)}), bf16[8,2,32,768]{3,2,1,0:T(8,128)(2,1)S(1)}, u32[]{:S(2)}, u32[]{:S(2)}) async-start(bf16[8,2,32,768]{3,2,1,0:T(8,128)(2,1)} %pad_maximum_fusion), calls=%async_computation.1 | async-start | bytes 1572864 | tf_op jit(solution)/shard_map/all_to_all | solution.py:254
  24.0 30.4 %copy-start = (bf16[512,768]{1,0:T(8,128)(2,1)S(1)}, bf16[512,768]{1,0:T(8,128)(2,1)}, u32[]{:S(2)}) copy-start(bf16[512,768]{1,0:T(8,128)(2,1)} %ck_ref.3) | copy-start | bytes 2359300
  24.0 30.4 %collective-permute-start.1 = (bf16[256,768]{1,0:T(8,128)(2,1)S(1)}, bf16[256,768]{1,0:T(8,128)(2,1)S(1)}, u32[]{:S(2)}, u32[]{:S(2)}) collective-permute-start(bf16[256,768]{1,0:T(8,128)(2,1)S(1)} %bitcast.27), channel_id=1, source_target_pairs={{8,0},{16,8},{24,16},{32,24},{40,32},{48,40},{56,48},{64,56},{72,6... | collective-permute-start | bytes 1179656 | tf_op jit(solution)/shard_map/ppermute | solution.py:241
  25.5 29.0 %collective-permute-start = (bf16[256,768]{1,0:T(8,128)(2,1)S(1)}, bf16[256,768]{1,0:T(8,128)(2,1)}, u32[]{:S(2)}, u32[]{:S(2)}) collective-permute-start(bf16[256,768]{1,0:T(8,128)(2,1)S(1)} %bitcast.28), channel_id=1, source_target_pairs={{0,8},{8,16},{16,24},{24,32},{32,40},{40,48},{48,56},{56,64},{64,7... | collective-permute-start | bytes 1179656 | tf_op jit(solution)/shard_map/ppermute | solution.py:241
  30.8 11.7 %collective-permute-start.3 = (bf16[112,768]{1,0:T(8,128)(2,1)S(1)}, bf16[112,768]{1,0:T(8,128)(2,1)}, u32[]{:S(2)}, u32[]{:S(2)}) collective-permute-start(bf16[112,768]{1,0:T(8,128)(2,1)S(1)} %slice.7), channel_id=1, source_target_pairs={{120,0},{248,128},{376,256},{128,248},{256,376},{384,504},{121,1},... | collective-permute-start | bytes 516104 | tf_op jit(solution)/shard_map/ppermute | solution.py:241
  36.0 18.5 %copy-start.3 = (s32[128]{0:T(128)S(1)}, s32[128]{0:T(128)}, u32[]{:S(2)}) copy-start(s32[128]{0:T(128)} %reached_ref.3) | copy-start | bytes 1540
  36.0 17.8 %collective-permute-start.2 = (bf16[144,768]{1,0:T(8,128)(2,1)}, bf16[144,768]{1,0:T(8,128)(2,1)S(1)}, u32[]{:S(2)}, u32[]{:S(2)}) collective-permute-start(bf16[144,768]{1,0:T(8,128)(2,1)} %slice.6), channel_id=1, source_target_pairs={{120,128},{248,256},{376,384},{128,120},{256,248},{384,376},{121,1... | collective-permute-start | bytes 663560 | tf_op jit(solution)/shard_map/ppermute | solution.py:241
  42.5 12.0 %collective-permute-start.4 = (bf16[112,768]{1,0:T(8,128)(2,1)}, bf16[112,768]{1,0:T(8,128)(2,1)}, u32[]{:S(2)}, u32[]{:S(2)}) collective-permute-start(bf16[112,768]{1,0:T(8,128)(2,1)} %collective-permute-done.3), channel_id=1, source_target_pairs={{0,128},{128,256},{256,384},{248,120},{376,248},{504,376},{1,129},... | collective-permute-start | bytes 516104 | tf_op jit(solution)/shard_map/ppermute | solution.py:241
  63.9 43.8 %collective-permute-start.5 = (bf16[272,768]{1,0:T(8,128)(2,1)S(1)}, bf16[272,768]{1,0:T(8,128)(2,1)S(1)}, u32[]{:S(2)}, u32[]{:S(2)}) collective-permute-start(bf16[272,768]{1,0:T(8,128)(2,1)S(1)} %get-tuple-element.17), channel_id=1, source_target_pairs={{0,8},{8,16},{16,24},{24,32},{32,40},{40,48},{48,56},{56,64},{64,7... | collective-permute-start | bytes 1253384 | tf_op jit(solution)/shard_map/ppermute | solution.py:241
  65.2 42.5 %collective-permute-start.6 = (bf16[272,768]{1,0:T(8,128)(2,1)S(1)}, bf16[272,768]{1,0:T(8,128)(2,1)S(1)}, u32[]{:S(2)}, u32[]{:S(2)}) collective-permute-start(bf16[272,768]{1,0:T(8,128)(2,1)S(1)} %get-tuple-element.18), channel_id=1, source_target_pairs={{8,0},{16,8},{24,16},{32,24},{40,32},{48,40},{56,48},{64,56},{72,6... | collective-permute-start | bytes 1253384 | tf_op jit(solution)/shard_map/ppermute | solution.py:241
  66.5 24.6 %collective-permute-start.8 = (bf16[112,768]{1,0:T(8,128)(2,1)S(1)}, bf16[112,768]{1,0:T(8,128)(2,1)S(1)}, u32[]{:S(2)}, u32[]{:S(2)}) collective-permute-start(bf16[112,768]{1,0:T(8,128)(2,1)S(1)} %get-tuple-element.20), channel_id=1, source_target_pairs={{120,0},{248,128},{376,256},{128,248},{256,376},{384,504},{121,1},... | collective-permute-start | bytes 516104 | tf_op jit(solution)/shard_map/ppermute | solution.py:241
  87.7 20.0 %copy-start.2 = (f32[6144]{0:T(1024)S(1)}, f32[6144]{0:T(1024)}, u32[]{:S(2)}) copy-start(f32[6144]{0:T(1024)} %param.15) | copy-start | bytes 73732
  87.7 19.9 %collective-permute-start.7 = (bf16[160,768]{1,0:T(8,128)(2,1)S(1)}, bf16[160,768]{1,0:T(8,128)(2,1)S(1)}, u32[]{:S(2)}, u32[]{:S(2)}) collective-permute-start(bf16[160,768]{1,0:T(8,128)(2,1)S(1)} %get-tuple-element.19), channel_id=1, source_target_pairs={{120,128},{248,256},{376,384},{128,120},{256,248},{384,376},{121,1... | collective-permute-start | bytes 737288 | tf_op jit(solution)/shard_map/ppermute | solution.py:241
  91.1 16.6 %collective-permute-start.9 = (bf16[112,768]{1,0:T(8,128)(2,1)S(1)}, bf16[112,768]{1,0:T(8,128)(2,1)S(1)}, u32[]{:S(2)}, u32[]{:S(2)}) collective-permute-start(bf16[112,768]{1,0:T(8,128)(2,1)S(1)} %collective-permute-done.8), channel_id=1, source_target_pairs={{0,128},{128,256},{256,384},{248,120},{376,248},{504,376},{1,129},... | collective-permute-start | bytes 516104 | tf_op jit(solution)/shard_map/ppermute | solution.py:241

commit v3 on v2

--- a/solution.py
+++ b/solution.py
@@ -46,7 +46,7 @@
     tile_count = pattern_ref.shape[0]
     for row, rel in enumerate(rel_tiles):
         for t in range(own_tiles):
-            near = 0.0 if abs(rel - t) <= 2 else NEGATIVE
+            near = jnp.where(jnp.abs(rel - t) <= 2, 0.0, NEGATIVE)
             bias_ref[row, :, t * TILE : (t + 1) * TILE] = jnp.full((8, TILE), near, jnp.float32)
         for u in range(cached_tiles):
             bias = tile_bias(
@@ -107,55 +107,74 @@
         put(t, None, stats)
 
 
+def put_partial(o_ref, rows, t, cols, value):
+    if cols is None:
+        for i, piece in enumerate(pieces(value)):
+            o_ref[rows:, (3 * t + i) * TILE : (3 * t + i + 1) * TILE] = piece
+    else:
+        o_ref[t * TILE : (t + 1) * TILE, cols] = value.astype(jnp.bfloat16)
+
+
 def far_kernel(
+    pattern_ref, reached_ref, below_ref, above_ref, kv_ref, ck_ref, cv_ref, to_below_ref, to_above_ref, bias_ref
+):
+    own = kv_ref.shape[0] * kv_ref.shape[2] // TILE
+    at = lax.rem(lax.axis_index("ctx"), PLANE)
+    sides = ((below_ref, to_below_ref, at > 0, -own), (above_ref, to_above_ref, at < PLANE - 1, own))
+    for q_ref, o_ref, inside, base in sides:
+
+        @pl.when(inside)
+        def _(q_ref=q_ref, o_ref=o_ref, base=base):
+            rel = tuple(base + t for t in range(own))
+            fill_bias(bias_ref, pattern_ref, reached_ref, rel, own, ck_ref.shape[0] // TILE)
+
+            def load(t, cols):
+                return q_ref[t * TILE : (t + 1) * TILE, cols]
+
+            put = functools.partial(put_partial, o_ref, own * TILE)
+            attend_all(load, kv_ref, ck_ref, cv_ref, bias_ref, 0, put)
+
+
+def jump_kernel(
     pattern_ref,
     reached_ref,
-    below_ref,
-    above_ref,
     direct_ref,
     swapped_ref,
     kv_ref,
     ck_ref,
     cv_ref,
-    to_below_ref,
-    to_above_ref,
     to_direct_ref,
     to_swapped_ref,
     bias_ref,
+    o_ref,
 ):
     own = kv_ref.shape[0] * kv_ref.shape[2] // TILE
-    rel = tuple(range(-own, 0)) + tuple(range(own, 2 * own))
-    fill_bias(bias_ref, pattern_ref, reached_ref, rel, own, ck_ref.shape[0] // TILE)
-    rows = own * TILE
     near = direct_ref.shape[0]
     at = lax.rem(lax.axis_index("ctx"), PLANE)
-    sides = ((below_ref, to_below_ref, at == 0), (above_ref, to_above_ref, at == PLANE - 1))
-    for side, (q_ref, o_ref, jumps) in enumerate(sides):
-
-        def load(t, cols, q_ref=q_ref, jumps=jumps):
-            low, high = t * TILE, (t + 1) * TILE
-            if high <= near:
-                jumped = direct_ref[low:high, cols]
-            elif low >= near:
-                jumped = swapped_ref[low - near : high - near, cols]
-            else:
-                jumped = jnp.concatenate([direct_ref[low:, cols], swapped_ref[: high - near, cols]], axis=0)
-            return jnp.where(jumps, jumped, q_ref[low:high, cols])
-
-        def put(t, cols, value, o_ref=o_ref):
-            if cols is None:
-                for i, piece in enumerate(pieces(value)):
-                    o_ref[rows:, (3 * t + i) * TILE : (3 * t + i + 1) * TILE] = piece
-            else:
-                o_ref[t * TILE : (t + 1) * TILE, cols] = value.astype(jnp.bfloat16)
-
-        attend_all(load, kv_ref, ck_ref, cv_ref, bias_ref, side * own, put)
-
-        @pl.when(jumps)
-        def _(o_ref=o_ref):
-            direct = to_direct_ref.shape[0]
-            to_direct_ref[...] = o_ref[:direct]
-            to_swapped_ref[...] = o_ref[direct:]
+
+    @pl.when(jnp.logical_or(at == 0, at == PLANE - 1))
+    def _():
+        base = jnp.where(at == 0, -own, own)
+        rel = tuple(base + t for t in range(own))
+        fill_bias(bias_ref, pattern_ref, reached_ref, rel, own, ck_ref.shape[0] // TILE)
+
+        def load(t, cols):
+            return joined(direct_ref, swapped_ref, near, t, cols)
+
+        put = functools.partial(put_partial, o_ref, own * TILE)
+        attend_all(load, kv_ref, ck_ref, cv_ref, bias_ref, 0, put)
+        direct = to_direct_ref.shape[0]
+        to_direct_ref[...] = o_ref[:direct]
+        to_swapped_ref[...] = o_ref[direct:]
+
+
+def joined(direct_ref, swapped_ref, near, t, cols):
+    low, high = t * TILE, (t + 1) * TILE
+    if high <= near:
+        return direct_ref[low:high, cols]
+    if low >= near:
+        return swapped_ref[low - near : high - near, cols]
+    return jnp.concatenate([direct_ref[low:, cols], swapped_ref[: high - near, cols]], axis=0)
 
 
 def own_kernel(pattern_ref, reached_ref, q_ref, kv_ref, ck_ref, cv_ref, o_ref, stats_ref, bias_ref):
@@ -199,13 +218,7 @@
         mine, low, high = mine * total, low * total, high * total
         for h in range(heads):
             cols = slice(h * HD, (h + 1) * HD)
-            start, stop = t * TILE, (t + 1) * TILE
-            if stop <= near:
-                jumped = direct_ref[start:stop, cols]
-            elif start >= near:
-                jumped = swapped_ref[start - near : stop - near, cols]
-            else:
-                jumped = jnp.concatenate([direct_ref[start:, cols], swapped_ref[: stop - near, cols]], axis=0)
+            jumped = joined(direct_ref, swapped_ref, near, t, cols)
             gate = gate_ref[pl.ds(head * heads + h, 1), :]
             mixed = o_ref[here, cols] * mine[:, h : h + 1]
             mixed = mixed + jnp.where(first, jumped, low_ref[here, cols]).astype(jnp.float32) * low[:, h : h + 1]
@@ -255,21 +268,35 @@
 
     keys_seen = rows + cached
     partial = rows + 16
-    shapes = [partial, partial, partial - SWAPPED, SWAPPED]
-    to_below, to_above, to_direct, to_swapped = pl.pallas_call(
+
+    def shapes(*counts):
+        return tuple(jax.ShapeDtypeStruct((n, width), jnp.bfloat16) for n in counts)
+
+    bias = pltpu.VMEM((own, 8, keys_seen), jnp.float32)
+    to_below, to_above = pl.pallas_call(
         far_kernel,
-        out_shape=tuple(jax.ShapeDtypeStruct((n, width), jnp.bfloat16) for n in shapes),
-        in_specs=[smem(), smem()] + [vmem()] * 7,
-        out_specs=(vmem(),) * 4,
-        scratch_shapes=[pltpu.VMEM((2 * own, 8, keys_seen), jnp.float32)],
+        out_shape=shapes(partial, partial),
+        in_specs=[smem(), smem()] + [vmem()] * 5,
+        out_specs=(vmem(),) * 2,
+        scratch_shapes=[bias],
         cost_estimate=attention_cost(2 * own, rows, cached, width),
         compiler_params=pltpu.CompilerParams(vmem_limit_bytes=LIMIT),
         name="far",
-    )(pattern, reached, from_below, from_above, direct, swapped, kv, cache_keys, cache_values)
+    )(pattern, reached, from_below, from_above, kv, cache_keys, cache_values)
+    got_high = shift(to_below, down)
+    got_low = shift(to_above, up)
+    to_direct, to_swapped = pl.pallas_call(
+        jump_kernel,
+        out_shape=shapes(partial - SWAPPED, SWAPPED),
+        in_specs=[smem(), smem()] + [vmem()] * 5,
+        out_specs=(vmem(),) * 2,
+        scratch_shapes=[bias, pltpu.VMEM((partial, width), jnp.bfloat16)],
+        cost_estimate=attention_cost(own, rows, cached, width),
+        compiler_params=pltpu.CompilerParams(vmem_limit_bytes=LIMIT),
+        name="jump",
+    )(pattern, reached, direct, swapped, kv, cache_keys, cache_values)
     swapped = shift(to_swapped, swap)
     direct = shift(to_direct, straight)
-    got_high = shift(to_below, down)
-    got_low = shift(to_above, up)
     swapped = shift(swapped, onward)
     mine, stats = pl.pallas_call(
         own_kernel,

time: 134 us -> 127 us (0.948)
  starting transfers between devices: 65.9 us -> 52.3 us
  waiting for transfers between devices: 23 us -> 27.3 us
  Pallas kernels: 15.7 us -> 17.4 us
    ppermute x10, starting transfers between devices: 56.2 us -> 42.6 us  [shift(): return lax.ppermute(x, 'ctx', pairs)]
    all_to_all x1, waiting for transfers between devices: 0.01 us -> 6.94 us  [local(): kv = lax.all_to_all(kv, 'head', split_axis=0, concat_axis=0, tiled=True)]
    ppermute x10, waiting for transfers between devices: 11.5 us -> 8.88 us  [shift(): return lax.ppermute(x, 'ctx', pairs)]
    pallas_call x1 -> x2, Pallas kernels: 9.38 us -> 11.1 us  [the longest x1 5.56 us: local(): pl.pallas_call(jump_kernel, out_shape=shapes(partial - SWAPPED, SWAPPED),...]
  transfers between devices with their start and end apart: 12 -> 12, of which waited for: 5 -> 5; matrix products, arithmetic and copies ran while one was open for 1% -> 1% of each run, Pallas kernels for 4% -> 13%
where the time goes in v3:
time: 127 us; the launch traced here: 126 us
  starting transfers between devices  52.3 us (41%)
  waiting for transfers between devices  27.3 us (21%)
  blocking collectives  25.1 us (20%)
  Pallas kernels  17.4 us (14%)
  local copies, waits for them, and re-layouts  2.8 us (2%)
    ppermute x10, starting transfers between devices, shift(): return lax.ppermute(x, 'ctx', pairs)  42.6 us
    all_to_all x1, blocking collectives, local(): lax.all_to_all(out.reshape(split, part, width), 'head', split_axis=0, con...  25.1 us
    all_to_all x1, waiting for transfers between devices, local(): lax.all_to_all(blocks(queries), 'head', split_axis=0, concat_axis=0, tile...  11.5 us
    ppermute x10, waiting for transfers between devices, shift(): return lax.ppermute(x, 'ctx', pairs)  8.88 us
    all_to_all x1, waiting for transfers between devices, local(): kv = lax.all_to_all(kv, 'head', split_axis=0, concat_axis=0, tiled=True)  6.94 us
    all_to_all x1, starting transfers between devices, local(): lax.all_to_all(blocks(queries), 'head', split_axis=0, concat_axis=0, tile...  6.03 us
    pallas_call x1, Pallas kernels, local(): pl.pallas_call(jump_kernel, out_shape=shapes(partial - SWAPPED, SWAPPED),...  5.56 us
    pallas_call x1, Pallas kernels, local(): pl.pallas_call(own_kernel, out_shape=(jax.ShapeDtypeStruct((rows, width),...  5.5 us
  transfers between devices with their start and end apart: 12, of which 5 were waited for; matrix products, arithmetic and copies ran while one was open for 1% of the time, Pallas kernels for 13%

profile of v3, /device:TPU:128, one launch (start us, length us, event | category | flops | bytes accessed | tf_op | source)
XLA Modules:
  0.0 126.0 jit_solution(987589843891290764)
XLA Ops:
  0.0 1.8 %copy.28 = bf16[4,8,8,768]{3,2,0,1:T(8,128)(2,1)} copy(bf16[4,8,8,768]{3,2,1,0:T(8,128)(2,1)} %bitcast.35) | data formatting | bytes 786432 | tf_op jit(solution)/shard_map/reshape | solution.py:257
  1.8 0.0 copy-start.4
  1.8 0.0 copy-start.5
  1.8 6.0 %all-to-all-start = ((bf16[8,32,768]{2,1,0:T(8,128)(2,1)}), bf16[8,32,768]{2,1,0:T(8,128)(2,1)S(1)}, u32[]{:S(2)}, u32[]{:S(2)}) async-start(bf16[8,32,768]{2,1,0:T(8,128)(2,1)} %bitcast.26), calls=%async_computation | async-start | bytes 786432 | tf_op jit(solution)/shard_map/all_to_all | solution.py:259
  7.8 0.0 copy-done.4
  7.8 0.0 copy-done.5
  7.8 0.1 bitcast_bitcast_fusion
  7.9 1.0 pad_maximum_fusion
  8.9 11.5 %all-to-all-done = bf16[8,32,768]{2,1,0:T(8,128)(2,1)S(1)} async-done(((bf16[8,32,768]{2,1,0:T(8,128)(2,1)}), bf16[8,32,768]{2,1,0:T(8,128)(2,1)S(1)}, u32[]{:S(2)}, u32[]{:S(2)}) %all-to-all-start) | async-done | bytes 393248 | tf_op jit(solution)/shard_map/all_to_all | solution.py:259
  20.3 0.0 copy-start.6
  20.3 0.0 copy-start.1
  20.3 3.7 %all-to-all-start.1 = ((bf16[8,2,32,768]{3,2,1,0:T(8,128)(2,1)}), bf16[8,2,32,768]{3,2,1,0:T(8,128)(2,1)S(1)}, u32[]{:S(2)}, u32[]{:S(2)}) async-start(bf16[8,2,32,768]{3,2,1,0:T(8,128)(2,1)} %pad_maximum_fusion), calls=%async_computation.1 | async-start | bytes 1572864 | tf_op jit(solution)/shard_map/all_to_all | solution.py:267
  24.0 0.0 copy-start
  24.0 4.4 %collective-permute-start = (bf16[256,768]{1,0:T(8,128)(2,1)S(1)}, bf16[256,768]{1,0:T(8,128)(2,1)}, u32[]{:S(2)}, u32[]{:S(2)}) collective-permute-start(bf16[256,768]{1,0:T(8,128)(2,1)S(1)} %bitcast.27), channel_id=1, source_target_pairs={{0,8},{8,16},{16,24},{24,32},{32,40},{40,48},{48,56},{56,64},{64,7... | collective-permute-start | bytes 1179656 | tf_op jit(solution)/shard_map/ppermute | solution.py:254
  28.4 1.3 %collective-permute-start.1 = (bf16[256,768]{1,0:T(8,128)(2,1)S(1)}, bf16[256,768]{1,0:T(8,128)(2,1)}, u32[]{:S(2)}, u32[]{:S(2)}) collective-permute-start(bf16[256,768]{1,0:T(8,128)(2,1)S(1)} %bitcast.28), channel_id=1, source_target_pairs={{8,0},{16,8},{24,16},{32,24},{40,32},{48,40},{56,48},{64,56},{72,6... | collective-permute-start | bytes 1179656 | tf_op jit(solution)/shard_map/ppermute | solution.py:254
  29.7 8.2 %collective-permute-start.5 = (bf16[112,768]{1,0:T(8,128)(2,1)S(1)}, bf16[112,768]{1,0:T(8,128)(2,1)}, u32[]{:S(2)}, u32[]{:S(2)}) collective-permute-start(bf16[112,768]{1,0:T(8,128)(2,1)S(1)} %slice.7), channel_id=1, source_target_pairs={{120,0},{248,128},{376,256},{128,248},{256,376},{384,504},{121,1},... | collective-permute-start | bytes 516104 | tf_op jit(solution)/shard_map/ppermute | solution.py:254
  37.9 0.0 copy-start.3
  37.9 1.9 %collective-permute-start.4 = (bf16[144,768]{1,0:T(8,128)(2,1)S(1)}, bf16[144,768]{1,0:T(8,128)(2,1)S(1)}, u32[]{:S(2)}, u32[]{:S(2)}) collective-permute-start(bf16[144,768]{1,0:T(8,128)(2,1)S(1)} %slice.6), channel_id=1, source_target_pairs={{120,128},{248,256},{376,384},{128,120},{256,248},{384,376},{121,1... | collective-permute-start | bytes 663560 | tf_op jit(solution)/shard_map/ppermute | solution.py:254
  39.9 2.5 %collective-permute-done.5 = bf16[112,768]{1,0:T(8,128)(2,1)} collective-permute-done((bf16[112,768]{1,0:T(8,128)(2,1)S(1)}, bf16[112,768]{1,0:T(8,128)(2,1)}, u32[]{:S(2)}, u32[]{:S(2)}) %collective-permute-start.5) | collective-permute-done | bytes 172064 | tf_op jit(solution)/shard_map/ppermute | solution.py:254
  42.4 6.6 %collective-permute-start.6 = (bf16[112,768]{1,0:T(8,128)(2,1)}, bf16[112,768]{1,0:T(8,128)(2,1)S(1)}, u32[]{:S(2)}, u32[]{:S(2)}) collective-permute-start(bf16[112,768]{1,0:T(8,128)(2,1)} %collective-permute-done.5), channel_id=1, source_target_pairs={{0,128},{128,256},{256,384},{248,120},{376,248},{504,376},{1,129},... | collective-permute-start | bytes 516104 | tf_op jit(solution)/shard_map/ppermute | solution.py:254
  48.9 0.0 copy-done.6
  48.9 0.1 copy.17.pattern_ref
  49.1 0.0 collective-permute-done.below_ref
  49.1 0.0 collective-permute-done.1.above_ref
  49.1 6.9 %all-to-all-done.1.kv_ref = bf16[8,2,32,768]{3,2,1,0:T(8,128)(2,1)S(1)} async-done(((bf16[8,2,32,768]{3,2,1,0:T(8,128)(2,1)}), bf16[8,2,32,768]{3,2,1,0:T(8,128)(2,1)S(1)}, u32[]{:S(2)}, u32[]{:S(2)}) %all-to-all-start.1) | async-done | bytes 786464 | tf_op jit(solution)/shard_map/all_to_all | solution.py:267
  56.0 0.0 copy-done.1
  56.0 0.0 copy-done
  56.0 0.0 copy-done.3
  56.0 5.5 %far.1 = (bf16[272,768]{1,0:T(8,128)(2,1)S(1)}, bf16[272,768]{1,0:T(8,128)(2,1)S(1)}) custom-call(s32[128,4]{1,0:T(8,128)S(1)} %copy.17.pattern_ref, s32[128]{0:T(128)S(1)} %copy-done.3, bf16[256,768]{1,0:T(8,128)(2,1)} %collective-permute-done.below_ref, bf16[256,768]{1,0:T(8,128)(2,1)} %collective-permute-done.1.above_ref, ...), custom_call_target="tpu_custom_call" | custom-call | flops 1207959552 | bytes 2359296 | tf_op jit(solution)/shard_map/far/pallas_call | solution.py:276
  61.5 1.3 %collective-permute-start.2 = (bf16[272,768]{1,0:T(8,128)(2,1)S(1)}, bf16[272,768]{1,0:T(8,128)(2,1)S(1)}, u32[]{:S(2)}, u32[]{:S(2)}) collective-permute-start(bf16[272,768]{1,0:T(8,128)(2,1)S(1)} %get-tuple-element.17), channel_id=1, source_target_pairs={{0,8},{8,16},{16,24},{24,32},{32,40},{40,48},{48,56},{56,64},{64,7... | collective-permute-start | bytes 1253384 | tf_op jit(solution)/shard_map/ppermute | solution.py:254
  62.8 1.3 %collective-permute-start.3 = (bf16[272,768]{1,0:T(8,128)(2,1)S(1)}, bf16[272,768]{1,0:T(8,128)(2,1)S(1)}, u32[]{:S(2)}, u32[]{:S(2)}) collective-permute-start(bf16[272,768]{1,0:T(8,128)(2,1)S(1)} %get-tuple-element.18), channel_id=1, source_target_pairs={{8,0},{16,8},{24,16},{32,24},{40,32},{48,40},{56,48},{64,56},{72,6... | collective-permute-start | bytes 1253384 | tf_op jit(solution)/shard_map/ppermute | solution.py:254
  64.1 0.0 collective-permute-done.4.direct_ref
  64.1 0.0 collective-permute-done.6.swapped_ref
  64.2 5.6 %jump.1 = (bf16[160,768]{1,0:T(8,128)(2,1)S(1)}, bf16[112,768]{1,0:T(8,128)(2,1)S(1)}) custom-call(s32[128,4]{1,0:T(8,128)S(1)} %copy.17.pattern_ref, s32[128]{0:T(128)S(1)} %copy-done.3, bf16[144,768]{1,0:T(8,128)(2,1)S(1)} %collective-permute-done.4.direct_ref, bf16[112,768]{1,0:T(8,128)(2,1)S(1)} %collective-permute-done.6.swapped_ref, ...), custom_call_target="tpu_custom_call" | custom-call | flops 603979776 | bytes 2359296 | tf_op jit(solution)/shard_map/jump/pallas_call | solution.py:288
  69.7 9.7 %collective-permute-start.8 = (bf16[112,768]{1,0:T(8,128)(2,1)S(1)}, bf16[112,768]{1,0:T(8,128)(2,1)S(1)}, u32[]{:S(2)}, u32[]{:S(2)}) collective-permute-start(bf16[112,768]{1,0:T(8,128)(2,1)S(1)} %get-tuple-element.20), channel_id=1, source_target_pairs={{120,0},{248,128},{376,256},{128,248},{256,376},{384,504},{121,1},... | collective-permute-start | bytes 516104 | tf_op jit(solution)/shard_map/ppermute | solution.py:254
  79.4 0.0 copy-start.2
  79.4 2.0 %collective-permute-start.7 = (bf16[160,768]{1,0:T(8,128)(2,1)S(1)}, bf16[160,768]{1,0:T(8,128)(2,1)S(1)}, u32[]{:S(2)}, u32[]{:S(2)}) collective-permute-start(bf16[160,768]{1,0:T(8,128)(2,1)S(1)} %get-tuple-element.19), channel_id=1, source_target_pairs={{120,128},{248,256},{376,384},{128,120},{256,248},{384,376},{121,1... | collective-permute-start | bytes 737288 | tf_op jit(solution)/shard_map/ppermute | solution.py:254
  81.4 1.4 %collective-permute-done.8 = bf16[112,768]{1,0:T(8,128)(2,1)S(1)} collective-permute-done((bf16[112,768]{1,0:T(8,128)(2,1)S(1)}, bf16[112,768]{1,0:T(8,128)(2,1)S(1)}, u32[]{:S(2)}, u32[]{:S(2)}) %collective-permute-start.8) | collective-permute-done | bytes 172064 | tf_op jit(solution)/shard_map/ppermute | solution.py:254
  82.8 6.0 %collective-permute-start.9 = (bf16[112,768]{1,0:T(8,128)(2,1)S(1)}, bf16[112,768]{1,0:T(8,128)(2,1)S(1)}, u32[]{:S(2)}, u32[]{:S(2)}) collective-permute-start(bf16[112,768]{1,0:T(8,128)(2,1)S(1)} %collective-permute-done.8), channel_id=1, source_target_pairs={{0,128},{128,256},{256,384},{248,120},{376,248},{504,376},{1,129},... | collective-permute-start | bytes 516104 | tf_op jit(solution)/shard_map/ppermute | solution.py:254
  88.8 5.5 %own.1 = (f32[256,768]{1,0:T(8,128)S(1)}, f32[256,128]{1,0:T(8,128)S(1)}) custom-call(s32[128,4]{1,0:T(8,128)S(1)} %copy.17.pattern_ref, s32[128]{0:T(128)S(1)} %copy-done.3, bf16[256,768]{1,0:T(8,128)(2,1)S(1)} %bitcast.31, bf16[8,2,32,768]{3,2,1,0:T(8,128)(2,1)S(1)} %all-to-all-done.1.kv_ref, bf16[512,768]{1,0:T(8,128)(2,1)S(1)} %copy-done, ...), custom_call_target="tpu_custom_call" | custom-call | flops 603979776 | bytes 2359296 | tf_op jit(solution)/shard_map/own/pallas_call | solution.py:301
  94.3 5.0 %collective-permute-done.7.direct_ref = bf16[160,768]{1,0:T(8,128)(2,1)S(1)} collective-permute-done((bf16[160,768]{1,0:T(8,128)(2,1)S(1)}, bf16[160,768]{1,0:T(8,128)(2,1)S(1)}, u32[]{:S(2)}, u32[]{:S(2)}) %collective-permute-start.7) | collective-permute-done | bytes 245792 | tf_op jit(solution)/shard_map/ppermute | solution.py:254
  99.3 0.0 collective-permute-done.9.swapped_ref
  99.3 0.0 collective-permute-done.2.low_ref
  99.3 0.0 collective-permute-done.3.high_ref
  99.3 0.0 copy-done.2
  99.3 0.8 mix.1
  100.1 25.1 %all_to_all.15 = bf16[8,32,768]{2,1,0:T(8,128)(2,1)S(1)} all-to-all(bf16[8,32,768]{2,1,0:T(8,128)(2,1)S(1)} %bitcast.32), channel_id=1, replica_groups=mesh['ctx'=64,'head'=8] {'head'}, dimensions={0} | all-to-all | bytes 786432 | tf_op jit(solution)/shard_map/all_to_all | solution.py:322
  125.3 0.8 copy.24
  (2 shorter events, 0.0 us)
Async XLA Ops:
  1.8 6.0 %copy-start.4 = (bf16[32,6144]{1,0:T(8,128)(2,1)S(1)}, bf16[32,6144]{1,0:T(8,128)(2,1)}, u32[]{:S(2)}) copy-start(bf16[32,6144]{1,0:T(8,128)(2,1)} %param.10) | copy-start | bytes 1179652
  1.8 6.0 %copy-start.5 = (bf16[32,6144]{1,0:T(8,128)(2,1)S(1)}, bf16[32,6144]{1,0:T(8,128)(2,1)}, u32[]{:S(2)}) copy-start(bf16[32,6144]{1,0:T(8,128)(2,1)} %param.9) | copy-start | bytes 1179652
  1.8 18.6 %all-to-all-start = ((bf16[8,32,768]{2,1,0:T(8,128)(2,1)}), bf16[8,32,768]{2,1,0:T(8,128)(2,1)S(1)}, u32[]{:S(2)}, u32[]{:S(2)}) async-start(bf16[8,32,768]{2,1,0:T(8,128)(2,1)} %bitcast.26), calls=%async_computation | async-start | bytes 786432 | tf_op jit(solution)/shard_map/all_to_all | solution.py:259
  20.3 28.6 %copy-start.6 = (s32[128,4]{0,1:T(4,128)S(1)}, s32[128,4]{0,1:T(4,128)}, u32[]{:S(2)}) copy-start(s32[128,4]{0,1:T(4,128)} %param.13) | copy-start | bytes 6148
  20.3 35.7 %copy-start.1 = (bf16[512,768]{1,0:T(8,128)(2,1)S(1)}, bf16[512,768]{1,0:T(8,128)(2,1)}, u32[]{:S(2)}) copy-start(bf16[512,768]{1,0:T(8,128)(2,1)} %cv_ref.5) | copy-start | bytes 2359300
  20.3 35.7 %all-to-all-start.1 = ((bf16[8,2,32,768]{3,2,1,0:T(8,128)(2,1)}), bf16[8,2,32,768]{3,2,1,0:T(8,128)(2,1)S(1)}, u32[]{:S(2)}, u32[]{:S(2)}) async-start(bf16[8,2,32,768]{3,2,1,0:T(8,128)(2,1)} %pad_maximum_fusion), calls=%async_computation.1 | async-start | bytes 1572864 | tf_op jit(solution)/shard_map/all_to_all | solution.py:267
  24.0 32.0 %copy-start = (bf16[512,768]{1,0:T(8,128)(2,1)S(1)}, bf16[512,768]{1,0:T(8,128)(2,1)}, u32[]{:S(2)}) copy-start(bf16[512,768]{1,0:T(8,128)(2,1)} %ck_ref.5) | copy-start | bytes 2359300
  24.0 25.0 %collective-permute-start = (bf16[256,768]{1,0:T(8,128)(2,1)S(1)}, bf16[256,768]{1,0:T(8,128)(2,1)}, u32[]{:S(2)}, u32[]{:S(2)}) collective-permute-start(bf16[256,768]{1,0:T(8,128)(2,1)S(1)} %bitcast.27), channel_id=1, source_target_pairs={{0,8},{8,16},{16,24},{24,32},{32,40},{40,48},{48,56},{56,64},{64,7... | collective-permute-start | bytes 1179656 | tf_op jit(solution)/shard_map/ppermute | solution.py:254
  28.4 20.6 %collective-permute-start.1 = (bf16[256,768]{1,0:T(8,128)(2,1)S(1)}, bf16[256,768]{1,0:T(8,128)(2,1)}, u32[]{:S(2)}, u32[]{:S(2)}) collective-permute-start(bf16[256,768]{1,0:T(8,128)(2,1)S(1)} %bitcast.28), channel_id=1, source_target_pairs={{8,0},{16,8},{24,16},{32,24},{40,32},{48,40},{56,48},{64,56},{72,6... | collective-permute-start | bytes 1179656 | tf_op jit(solution)/shard_map/ppermute | solution.py:254
  29.7 12.6 %collective-permute-start.5 = (bf16[112,768]{1,0:T(8,128)(2,1)S(1)}, bf16[112,768]{1,0:T(8,128)(2,1)}, u32[]{:S(2)}, u32[]{:S(2)}) collective-permute-start(bf16[112,768]{1,0:T(8,128)(2,1)S(1)} %slice.7), channel_id=1, source_target_pairs={{120,0},{248,128},{376,256},{128,248},{256,376},{384,504},{121,1},... | collective-permute-start | bytes 516104 | tf_op jit(solution)/shard_map/ppermute | solution.py:254
  37.9 18.1 %copy-start.3 = (s32[128]{0:T(128)S(1)}, s32[128]{0:T(128)}, u32[]{:S(2)}) copy-start(s32[128]{0:T(128)} %reached_ref.5) | copy-start | bytes 1540
  37.9 26.2 %collective-permute-start.4 = (bf16[144,768]{1,0:T(8,128)(2,1)S(1)}, bf16[144,768]{1,0:T(8,128)(2,1)S(1)}, u32[]{:S(2)}, u32[]{:S(2)}) collective-permute-start(bf16[144,768]{1,0:T(8,128)(2,1)S(1)} %slice.6), channel_id=1, source_target_pairs={{120,128},{248,256},{376,384},{128,120},{256,248},{384,376},{121,1... | collective-permute-start | bytes 663560 | tf_op jit(solution)/shard_map/ppermute | solution.py:254
  42.4 21.8 %collective-permute-start.6 = (bf16[112,768]{1,0:T(8,128)(2,1)}, bf16[112,768]{1,0:T(8,128)(2,1)S(1)}, u32[]{:S(2)}, u32[]{:S(2)}) collective-permute-start(bf16[112,768]{1,0:T(8,128)(2,1)} %collective-permute-done.5), channel_id=1, source_target_pairs={{0,128},{128,256},{256,384},{248,120},{376,248},{504,376},{1,129},... | collective-permute-start | bytes 516104 | tf_op jit(solution)/shard_map/ppermute | solution.py:254
  61.5 37.8 %collective-permute-start.2 = (bf16[272,768]{1,0:T(8,128)(2,1)S(1)}, bf16[272,768]{1,0:T(8,128)(2,1)S(1)}, u32[]{:S(2)}, u32[]{:S(2)}) collective-permute-start(bf16[272,768]{1,0:T(8,128)(2,1)S(1)} %get-tuple-element.17), channel_id=1, source_target_pairs={{0,8},{8,16},{16,24},{24,32},{32,40},{40,48},{48,56},{56,64},{64,7... | collective-permute-start | bytes 1253384 | tf_op jit(solution)/shard_map/ppermute | solution.py:254
  62.8 36.5 %collective-permute-start.3 = (bf16[272,768]{1,0:T(8,128)(2,1)S(1)}, bf16[272,768]{1,0:T(8,128)(2,1)S(1)}, u32[]{:S(2)}, u32[]{:S(2)}) collective-permute-start(bf16[272,768]{1,0:T(8,128)(2,1)S(1)} %get-tuple-element.18), channel_id=1, source_target_pairs={{8,0},{16,8},{24,16},{32,24},{40,32},{48,40},{56,48},{64,56},{72,6... | collective-permute-start | bytes 1253384 | tf_op jit(solution)/shard_map/ppermute | solution.py:254
  69.7 13.1 %collective-permute-start.8 = (bf16[112,768]{1,0:T(8,128)(2,1)S(1)}, bf16[112,768]{1,0:T(8,128)(2,1)S(1)}, u32[]{:S(2)}, u32[]{:S(2)}) collective-permute-start(bf16[112,768]{1,0:T(8,128)(2,1)S(1)} %get-tuple-element.20), channel_id=1, source_target_pairs={{120,0},{248,128},{376,256},{128,248},{256,376},{384,504},{121,1},... | collective-permute-start | bytes 516104 | tf_op jit(solution)/shard_map/ppermute | solution.py:254
  79.4 19.9 %copy-start.2 = (f32[6144]{0:T(1024)S(1)}, f32[6144]{0:T(1024)}, u32[]{:S(2)}) copy-start(f32[6144]{0:T(1024)} %param.15) | copy-start | bytes 73732
  79.4 19.9 %collective-permute-start.7 = (bf16[160,768]{1,0:T(8,128)(2,1)S(1)}, bf16[160,768]{1,0:T(8,128)(2,1)S(1)}, u32[]{:S(2)}, u32[]{:S(2)}) collective-permute-start(bf16[160,768]{1,0:T(8,128)(2,1)S(1)} %get-tuple-element.19), channel_id=1, source_target_pairs={{120,128},{248,256},{376,384},{128,120},{256,248},{384,376},{121,1... | collective-permute-start | bytes 737288 | tf_op jit(solution)/shard_map/ppermute | solution.py:254
  82.8 16.4 %collective-permute-start.9 = (bf16[112,768]{1,0:T(8,128)(2,1)S(1)}, bf16[112,768]{1,0:T(8,128)(2,1)S(1)}, u32[]{:S(2)}, u32[]{:S(2)}) collective-permute-start(bf16[112,768]{1,0:T(8,128)(2,1)S(1)} %collective-permute-done.8), channel_id=1, source_target_pairs={{0,128},{128,256},{256,384},{248,120},{376,248},{504,376},{1,129},... | collective-permute-start | bytes 516104 | tf_op jit(solution)/shard_map/ppermute | solution.py:254

commit v4 on v3

v4 whole, which is shorter than its diff:
```python
import functools
import math

import jax
import jax.numpy as jnp
from jax import lax
from jax.experimental import pallas as pl
from jax.experimental.pallas import tpu as pltpu
from jax.sharding import PartitionSpec as P


HD = 128
TILE = 128
REACH = 4
NEGATIVE = -1e30
LIMIT = 24 << 20
PLANE = 16
SIDE = 4
DETOUR = 80
LOG2E = math.log2(math.e)
NT = (((1,), (1,)), ((), ()))


def vmem():
    return pl.BlockSpec(memory_space=pltpu.VMEM)


def smem():
    return pl.BlockSpec(memory_space=pltpu.SMEM)


def times_named(pattern_ref, reached_ref, tile, cached_id):
    row = jnp.clip(tile, 0, pattern_ref.shape[0] - 1)
    used = reached_ref[row]
    times = jnp.int32(0)
    for slot in range(REACH):
        hit = jnp.logical_and(slot < used, pattern_ref[row, slot] == cached_id)
        times = times + jnp.where(hit, 1, 0)
    return times


def scores_of(q, k):
    return lax.dot_general(q, k, NT, preferred_element_type=jnp.float32) * (HD**-0.5 * LOG2E)


def pieces(lse):
    lse = jnp.transpose(lse)[:16]
    high = lse.astype(jnp.bfloat16)
    rest = lse - high.astype(jnp.float32)
    middle = rest.astype(jnp.bfloat16)
    low = (rest - middle.astype(jnp.float32)).astype(jnp.bfloat16)
    return high, middle, low


def whole(rows):
    rows = rows.astype(jnp.float32)
    lse = rows[:, :TILE] + rows[:, TILE : 2 * TILE] + rows[:, 2 * TILE :]
    return jnp.transpose(jnp.concatenate([lse] * (HD // 16), axis=0))


def attend_all(load, rel_tiles, refs, put):
    pattern_ref, reached_ref, kv_ref, ck_ref, cv_ref, peak_ref, total_ref, sum_ref = refs
    parts, _, part, width = kv_ref.shape
    rows = parts * part
    own, cached, heads = rows // TILE, ck_ref.shape[0] // TILE, width // HD
    ctx = lax.axis_index("ctx")
    lane = lax.broadcasted_iota(jnp.int32, (TILE, HD), 1)
    for t, rel in enumerate(rel_tiles):
        near = [abs(rel - i) <= 2 if isinstance(rel, int) else None for i in range(own)]
        kept = [i for i, ok in enumerate(near) if ok is not False]
        seen = slice(kept[0], kept[-1] + 1)
        low, high = seen.start * TILE, seen.stop * TILE
        bias = None
        if None in near:
            ok = [jnp.where(jnp.abs(rel - i) <= 2, 0.0, NEGATIVE) for i in range(own)]
            bias = jnp.concatenate([jnp.full((1, TILE), one, jnp.float32) for one in ok], axis=1)
        for h in range(heads):
            cols = slice(h * HD, (h + 1) * HD)
            k = kv_ref[:, 0, :, cols].reshape(rows, HD)[low:high]
            v = kv_ref[:, 1, :, cols].reshape(rows, HD)[low:high]
            scores = scores_of(load(t, cols), k)
            if bias is not None:
                scores = scores + bias
            peak = jnp.max(scores, axis=1, keepdims=True)
            expos = jnp.exp2(scores - peak)
            total = jnp.sum(expos, axis=1, keepdims=True)
            sum_ref[h] = jnp.dot(expos.astype(jnp.bfloat16), v, preferred_element_type=jnp.float32)
            peak_ref[h] = jnp.broadcast_to(peak, (TILE, HD))
            total_ref[h] = jnp.broadcast_to(total, (TILE, HD))
        for u in range(cached):
            times = times_named(pattern_ref, reached_ref, ctx * own + rel, ctx * cached + u)

            @pl.when(times > 0)
            def _(t=t, u=u, times=times):
                log = jnp.where(times == 2, 1.0, jnp.where(times == 3, math.log2(3.0), 0.0))
                log = jnp.where(times == 4, 2.0, log)
                there = slice(u * TILE, (u + 1) * TILE)
                for h in range(heads):
                    cols = slice(h * HD, (h + 1) * HD)
                    scores = scores_of(load(t, cols), ck_ref[there, cols]) + log
                    old = peak_ref[h]
                    peak = jnp.maximum(old, jnp.max(scores, axis=1, keepdims=True))
                    factor = jnp.exp2(old - peak)
                    expos = jnp.exp2(scores - peak)
                    peak_ref[h] = peak
                    total_ref[h] = total_ref[h] * factor + jnp.sum(expos, axis=1, keepdims=True)
                    more = jnp.dot(expos.astype(jnp.bfloat16), cv_ref[there, cols], preferred_element_type=jnp.float32)
                    sum_ref[h] = sum_ref[h] * factor + more

        stats = jnp.zeros((TILE, HD), jnp.float32)
        for h in range(heads):
            total = total_ref[h]
            put(t, slice(h * HD, (h + 1) * HD), sum_ref[h] / total)
            stats = jnp.where(lane == h, peak_ref[h] + jnp.log2(total), stats)
        put(t, None, stats)


def put_partial(o_ref, rows, t, cols, value):
    if cols is None:
        for i, piece in enumerate(pieces(value)):
            o_ref[rows:, (3 * t + i) * TILE : (3 * t + i + 1) * TILE] = piece
    else:
        o_ref[t * TILE : (t + 1) * TILE, cols] = value.astype(jnp.bfloat16)


def far_kernel(
    pattern_ref, reached_ref, below_ref, above_ref, kv_ref, ck_ref, cv_ref, to_below_ref, to_above_ref, *scratch
):
    own = kv_ref.shape[0] * kv_ref.shape[2] // TILE
    refs = (pattern_ref, reached_ref, kv_ref, ck_ref, cv_ref, *scratch)
    at = lax.rem(lax.axis_index("ctx"), PLANE)
    sides = ((below_ref, to_below_ref, at > 0, -own), (above_ref, to_above_ref, at < PLANE - 1, own))
    for q_ref, o_ref, inside, base in sides:

        @pl.when(inside)
        def _(q_ref=q_ref, o_ref=o_ref, base=base):
            def load(t, cols):
                return q_ref[t * TILE : (t + 1) * TILE, cols]

            put = functools.partial(put_partial, o_ref, own * TILE)
            attend_all(load, [base + t for t in range(own)], refs, put)


def jump_kernel(*args):
    pattern_ref, reached_ref, *given = args[:5]
    kv_ref, _, _ = args[5:8]
    taken, o_ref, refs = args[8:11], args[11], (pattern_ref, reached_ref, *args[5:8], *args[12:])
    own = kv_ref.shape[0] * kv_ref.shape[2] // TILE
    at = lax.rem(lax.axis_index("ctx"), PLANE)

    @pl.when(jnp.logical_or(at == 0, at == PLANE - 1))
    def _():
        base = jnp.where(at == 0, -own, own)

        def load(t, cols):
            return joined(given, slice(t * TILE, (t + 1) * TILE), cols)

        put = functools.partial(put_partial, o_ref, own * TILE)
        attend_all(load, [base + t for t in range(own)], refs, put)
        first = 0
        for ref in taken:
            ref[...] = o_ref[first : first + ref.shape[0]]
            first += ref.shape[0]


def joined(refs, rows, cols):
    found, first = [], 0
    for ref in refs:
        low, high = max(rows.start - first, 0), min(rows.stop - first, ref.shape[0])
        if low < high:
            found.append(ref[low:high, cols])
        first += ref.shape[0]
    return found[0] if len(found) == 1 else jnp.concatenate(found, axis=0)


def own_kernel(pattern_ref, reached_ref, q_ref, kv_ref, ck_ref, cv_ref, o_ref, stats_ref, *scratch):
    own = kv_ref.shape[0] * kv_ref.shape[2] // TILE

    def put(t, cols, value):
        rows = slice(t * TILE, (t + 1) * TILE)
        if cols is None:
            stats_ref[rows, :] = value
        else:
            o_ref[rows, cols] = value

    def load(t, cols):
        return q_ref[t * TILE : (t + 1) * TILE, cols]

    attend_all(load, list(range(own)), (pattern_ref, reached_ref, kv_ref, ck_ref, cv_ref, *scratch), put)


def mix_kernel(count, o_ref, stats_ref, low_ref, high_ref, part0_ref, part1_ref, part2_ref, gate_ref, out_ref):
    parts = (part0_ref, part1_ref, part2_ref)
    ctx = lax.axis_index("ctx")
    at = lax.rem(ctx, PLANE)
    first, last = at == 0, at == PLANE - 1
    head = lax.axis_index("head")
    rows, width = o_ref.shape
    heads = width // HD
    for t in range(rows // TILE):
        here = slice(t * TILE, (t + 1) * TILE)
        stat = slice(rows, rows + 16), slice(3 * t * TILE, 3 * (t + 1) * TILE)
        jumped = joined(parts, *stat)
        low = whole(jnp.where(first, jumped, low_ref[stat]))
        high = whole(jnp.where(last, jumped, high_ref[stat]))
        low = jnp.where(ctx > 0, low, NEGATIVE)
        high = jnp.where(ctx < count - 1, high, NEGATIVE)
        mine = stats_ref[here, :]
        peak = jnp.maximum(jnp.maximum(mine, low), high)
        mine, low, high = jnp.exp2(mine - peak), jnp.exp2(low - peak), jnp.exp2(high - peak)
        total = 1.0 / (mine + low + high)
        mine, low, high = mine * total, low * total, high * total
        for h in range(heads):
            cols = slice(h * HD, (h + 1) * HD)
            jumped = joined(parts, here, cols)
            gate = gate_ref[pl.ds(head * heads + h, 1), :]
            mixed = o_ref[here, cols] * mine[:, h : h + 1]
            mixed = mixed + jnp.where(first, jumped, low_ref[here, cols]).astype(jnp.float32) * low[:, h : h + 1]
            mixed = mixed + jnp.where(last, jumped, high_ref[here, cols]).astype(jnp.float32) * high[:, h : h + 1]
            out_ref[here, cols] = (mixed * gate).astype(jnp.bfloat16)


def attention_cost(tiles, rows, cached, width):
    pairs = tiles * TILE * (rows + cached)
    return pl.CostEstimate(
        flops=4 * pairs * width, bytes_accessed=4 * (rows + cached) * width, transcendentals=pairs * (width // HD)
    )


def local(queries, keys, values, cache_keys, cache_values, pattern, reached, gate):
    split = lax.axis_size("head")
    count = lax.axis_size("ctx")
    part, full = queries.shape
    width = full // split
    rows = part * split
    cached = cache_keys.shape[0]
    own = rows // TILE
    jumps = [(first - 1, first) for first in range(PLANE, count, PLANE)]
    corners = (PLANE - SIDE, SIDE - 1)
    up = [(i, i + 1) for i in range(count - 1) if (i + 1) % PLANE]
    down = [(b, a) for a, b in up]
    straight = jumps + [(b, a) for a, b in jumps]
    out, onward = [], []
    for rising, falling in (corners, corners[::-1]):
        ways = [(a, a + 1 - PLANE + rising, b) for a, b in jumps] + [(b, b + falling, a) for a, b in jumps]
        out.append([way[:2] for way in ways])
        onward.append([way[1:] for way in ways])

    def jump(x):
        return [shift(x[0], straight)] + [shift(shift(x[1 + i], out[i]), onward[i]) for i in range(2)]

    def shift(x, pairs):
        return lax.ppermute(x, "ctx", pairs)

    def blocks(x):
        return jnp.transpose(x.reshape(part, split, width), (1, 0, 2))

    q = lax.all_to_all(blocks(queries), "head", split_axis=0, concat_axis=0, tiled=True).reshape(rows, width)
    kv = jnp.stack([blocks(keys), blocks(values)], axis=1)
    q, kv = lax.optimization_barrier((q, kv))
    cuts = (rows - 2 * DETOUR, rows - DETOUR)
    jumped = jump([q[: cuts[0]], q[cuts[0] : cuts[1]], q[cuts[1] :]])
    from_below = shift(q, up)
    from_above = shift(q, down)
    kv = lax.all_to_all(kv, "head", split_axis=0, concat_axis=0, tiled=True)

    partial = rows + 16

    def shapes(*counts):
        return tuple(jax.ShapeDtypeStruct((n, width), jnp.bfloat16) for n in counts)

    running = [pltpu.VMEM((width // HD, TILE, HD), jnp.float32)] * 3
    to_below, to_above = pl.pallas_call(
        far_kernel,
        out_shape=shapes(partial, partial),
        in_specs=[smem(), smem()] + [vmem()] * 5,
        out_specs=(vmem(),) * 2,
        scratch_shapes=running,
        cost_estimate=attention_cost(2 * own, rows, cached, width),
        compiler_params=pltpu.CompilerParams(vmem_limit_bytes=LIMIT),
        name="far",
    )(pattern, reached, from_below, from_above, kv, cache_keys, cache_values)
    got_high = shift(to_below, down)
    got_low = shift(to_above, up)
    jumped = pl.pallas_call(
        jump_kernel,
        out_shape=shapes(partial - 2 * DETOUR, DETOUR, DETOUR),
        in_specs=[smem(), smem()] + [vmem()] * 6,
        out_specs=(vmem(),) * 3,
        scratch_shapes=[pltpu.VMEM((partial, width), jnp.bfloat16), *running],
        cost_estimate=attention_cost(own, rows, cached, width),
        compiler_params=pltpu.CompilerParams(vmem_limit_bytes=LIMIT),
        name="jump",
    )(pattern, reached, *jumped, kv, cache_keys, cache_values)
    jumped = jump(jumped)
    mine, stats = pl.pallas_call(
        own_kernel,
        out_shape=(
            jax.ShapeDtypeStruct((rows, width), jnp.float32),
            jax.ShapeDtypeStruct((rows, HD), jnp.float32),
        ),
        in_specs=[smem(), smem()] + [vmem()] * 4,
        out_specs=(vmem(), vmem()),
        scratch_shapes=running,
        cost_estimate=attention_cost(own, rows, cached, width),
        compiler_params=pltpu.CompilerParams(vmem_limit_bytes=LIMIT),
        name="own",
    )(pattern, reached, q, kv, cache_keys, cache_values)
    out = pl.pallas_call(
        functools.partial(mix_kernel, count),
        out_shape=jax.ShapeDtypeStruct((rows, width), jnp.bfloat16),
        in_specs=[vmem()] * 8,
        out_specs=vmem(),
        compiler_params=pltpu.CompilerParams(vmem_limit_bytes=LIMIT),
        name="mix",
    )(mine, stats, got_low, got_high, *jumped, gate.reshape(full // HD, HD))
    out = lax.all_to_all(out.reshape(split, part, width), "head", split_axis=0, concat_axis=0, tiled=True)
    return jnp.transpose(out, (1, 0, 2)).reshape(part, full)


def solution(mesh):
    tokens = P(("ctx", "head"), None)
    cached = P("ctx", "head")
    return jax.shard_map(
        local,
        mesh=mesh,
        in_specs=(tokens, tokens, tokens, cached, cached, P(), P(), P()),
        out_specs=tokens,
        check_vma=False,
    )
```

time: 127 us -> 132 us (1.039)
  the two profiles are of different devices: /device:TPU:128 before, /device:TPU:30 now
where the time goes in v4:
time: 132 us
  starting transfers between devices  66.6 us (50%)
  waiting for transfers between devices  24.7 us (19%)
  Pallas kernels  18.2 us (14%)
  blocking collectives  18.2 us (14%)
  local copies, waits for them, and re-layouts  2.79 us (2%)
    ppermute x14, starting transfers between devices, shift(): return lax.ppermute(x, 'ctx', pairs)  56.9 us
    all_to_all x1, blocking collectives, local(): lax.all_to_all(out.reshape(split, part, width), 'head', split_axis=0, con...  18.2 us
    ppermute x14, waiting for transfers between devices, shift(): return lax.ppermute(x, 'ctx', pairs)  13.3 us
    all_to_all x1, waiting for transfers between devices, local(): lax.all_to_all(blocks(queries), 'head', split_axis=0, concat_axis=0, tile...  11.4 us
    pallas_call x1, Pallas kernels, local(): pl.pallas_call(own_kernel, out_shape=(jax.ShapeDtypeStruct((rows, width),...  6.42 us
    all_to_all x1, starting transfers between devices, local(): lax.all_to_all(blocks(queries), 'head', split_axis=0, concat_axis=0, tile...  6.03 us
    pallas_call x1, Pallas kernels, local(): pl.pallas_call(far_kernel, out_shape=shapes(partial, partial), in_specs=[...  5.91 us
    pallas_call x1, Pallas kernels, local(): pl.pallas_call(jump_kernel, out_shape=shapes(partial - 2 * DETOUR, DETOUR...  4.99 us
  transfers between devices with their start and end apart: 16, of which 4 were waited for; matrix products, arithmetic and copies ran while one was open for 1% of the time, Pallas kernels for 13%

profile of v4, /device:TPU:30, one launch (start us, length us, event | category | flops | bytes accessed | tf_op | source)
XLA Modules:
  0.0 131.8 jit_solution(8807678898831792729)
XLA Ops:
  0.0 1.8 %copy.28 = bf16[4,8,8,768]{3,2,0,1:T(8,128)(2,1)} copy(bf16[4,8,8,768]{3,2,1,0:T(8,128)(2,1)} %bitcast.35) | data formatting | bytes 786432 | tf_op jit(solution)/shard_map/reshape | solution.py:256
  1.8 0.0 copy-start.4
  1.8 0.0 copy-start.5
  1.8 6.0 %all-to-all-start = ((bf16[8,32,768]{2,1,0:T(8,128)(2,1)}), bf16[8,32,768]{2,1,0:T(8,128)(2,1)S(1)}, u32[]{:S(2)}, u32[]{:S(2)}) async-start(bf16[8,32,768]{2,1,0:T(8,128)(2,1)} %bitcast.26), calls=%async_computation | async-start | bytes 786432 | tf_op jit(solution)/shard_map/all_to_all | solution.py:258
  7.8 0.0 copy-done.4
  7.8 0.0 copy-done.5
  7.8 0.1 bitcast_bitcast_fusion
  7.9 1.0 pad_maximum_fusion
  8.9 11.4 %all-to-all-done = bf16[8,32,768]{2,1,0:T(8,128)(2,1)S(1)} async-done(((bf16[8,32,768]{2,1,0:T(8,128)(2,1)}), bf16[8,32,768]{2,1,0:T(8,128)(2,1)S(1)}, u32[]{:S(2)}, u32[]{:S(2)}) %all-to-all-start) | async-done | bytes 393248 | tf_op jit(solution)/shard_map/all_to_all | solution.py:258
  20.3 0.0 copy-start.6
  20.3 0.0 copy-start.1
  20.3 3.7 %all-to-all-start.1 = ((bf16[8,2,32,768]{3,2,1,0:T(8,128)(2,1)}), bf16[8,2,32,768]{3,2,1,0:T(8,128)(2,1)S(1)}, u32[]{:S(2)}, u32[]{:S(2)}) async-start(bf16[8,2,32,768]{3,2,1,0:T(8,128)(2,1)} %pad_maximum_fusion), calls=%async_computation.1 | async-start | bytes 1572864 | tf_op jit(solution)/shard_map/all_to_all | solution.py:265
  24.0 0.0 copy-start
  24.0 1.4 %collective-permute-start = (bf16[256,768]{1,0:T(8,128)(2,1)S(1)}, bf16[256,768]{1,0:T(8,128)(2,1)}, u32[]{:S(2)}, u32[]{:S(2)}) collective-permute-start(bf16[256,768]{1,0:T(8,128)(2,1)S(1)} %bitcast.27), channel_id=1, source_target_pairs={{0,8},{8,16},{16,24},{24,32},{32,40},{40,48},{48,56},{56,64},{64,7... | collective-permute-start | bytes 1179656 | tf_op jit(solution)/shard_map/ppermute | solution.py:253
  25.5 5.3 %collective-permute-start.1 = (bf16[256,768]{1,0:T(8,128)(2,1)S(1)}, bf16[256,768]{1,0:T(8,128)(2,1)}, u32[]{:S(2)}, u32[]{:S(2)}) collective-permute-start(bf16[256,768]{1,0:T(8,128)(2,1)S(1)} %bitcast.28), channel_id=1, source_target_pairs={{8,0},{16,8},{24,16},{32,24},{40,32},{48,40},{56,48},{64,56},{72,6... | collective-permute-start | bytes 1179656 | tf_op jit(solution)/shard_map/ppermute | solution.py:253
  30.8 3.5 %collective-permute-start.5 = (bf16[80,768]{1,0:T(8,128)(2,1)S(1)}, bf16[80,768]{1,0:T(8,128)(2,1)S(1)}, u32[]{:S(2)}, u32[]{:S(2)}) collective-permute-start(bf16[80,768]{1,0:T(8,128)(2,1)S(1)} %get-tuple-element.24), channel_id=1, source_target_pairs={{120,96},{248,224},{376,352},{128,152},{256,280},{384,408},{121,97... | collective-permute-start | bytes 368648 | tf_op jit(solution)/shard_map/ppermute | solution.py:253
  34.3 1.9 %collective-permute-start.7 = (bf16[80,768]{1,0:T(8,128)(2,1)S(1)}, bf16[80,768]{1,0:T(8,128)(2,1)}, u32[]{:S(2)}, u32[]{:S(2)}) collective-permute-start(bf16[80,768]{1,0:T(8,128)(2,1)S(1)} %get-tuple-element.23), channel_id=1, source_target_pairs={{120,24},{248,152},{376,280},{128,224},{256,352},{384,480},{121,25... | collective-permute-start | bytes 368648 | tf_op jit(solution)/shard_map/ppermute | solution.py:253
  36.2 0.0 copy-done.6
  36.3 0.1 copy.17.pattern_ref.args_0_
  36.4 0.0 copy-start.3
  36.4 11.2 %collective-permute-start.4 = (bf16[96,768]{1,0:T(8,128)(2,1)S(1)}, bf16[96,768]{1,0:T(8,128)(2,1)S(1)}, u32[]{:S(2)}, u32[]{:S(2)}) collective-permute-start(bf16[96,768]{1,0:T(8,128)(2,1)S(1)} %slice.9), channel_id=1, source_target_pairs={{120,128},{248,256},{376,384},{128,120},{256,248},{384,376},{121,1... | collective-permute-start | bytes 442376 | tf_op jit(solution)/shard_map/ppermute | solution.py:253
  47.6 0.0 collective-permute-done.5
  47.6 1.3 collective-permute-start.6
  48.9 0.0 collective-permute-done.7
  48.9 1.3 collective-permute-start.8
  50.2 0.0 collective-permute-done.below_ref
  50.2 0.0 collective-permute-done.1.above_ref
  50.2 0.0 all-to-all-done.1.kv_ref.args_5_
  50.3 0.0 copy-done.1
  50.3 0.0 copy-done
  50.3 0.0 copy-done.3
  50.3 5.9 %far.1 = (bf16[272,768]{1,0:T(8,128)(2,1)S(1)}, bf16[272,768]{1,0:T(8,128)(2,1)S(1)}) custom-call(s32[128,4]{1,0:T(8,128)S(1)} %copy.17.pattern_ref.args_0_, s32[128]{0:T(128)S(1)} %copy-done.3, bf16[256,768]{1,0:T(8,128)(2,1)} %collective-permute-done.below_ref, bf16[256,768]{1,0:T(8,128)(2,1)} %collective-permute-done.1.above_ref, ...), custom_call_target="tpu_custom_call" | custom-call | flops 1207959552 | bytes 2359296 | tf_op jit(solution)/shard_map/far/pallas_call | solution.py:273
  56.2 1.3 collective-permute-start.2
  57.5 8.2 %collective-permute-start.3 = (bf16[272,768]{1,0:T(8,128)(2,1)S(1)}, bf16[272,768]{1,0:T(8,128)(2,1)S(1)}, u32[]{:S(2)}, u32[]{:S(2)}) collective-permute-start(bf16[272,768]{1,0:T(8,128)(2,1)S(1)} %get-tuple-element.19), channel_id=1, source_target_pairs={{8,0},{16,8},{24,16},{32,24},{40,32},{48,40},{56,48},{64,56},{72,6... | collective-permute-start | bytes 1253384 | tf_op jit(solution)/shard_map/ppermute | solution.py:253
  65.8 0.0 collective-permute-done.4.args_2_
  65.8 0.0 collective-permute-done.6.args_3_
  65.8 0.0 collective-permute-done.8.args_4_
  65.8 5.0 %jump.1 = (bf16[112,768]{1,0:T(8,128)(2,1)S(1)}, bf16[80,768]{1,0:T(8,128)(2,1)S(1)}, bf16[80,768]{1,0:T(8,128)(2,1)S(1)}) custom-call(s32[128,4]{1,0:T(8,128)S(1)} %copy.17.pattern_ref.args_0_, s32[128]{0:T(128)S(1)} %copy-done.3, bf16[96,768]{1,0:T(8,128)(2,1)S(1)} %collective-permute-done.4.args_2_, bf16[80,768]{1,0:T(8,128)(2,1)S(1)} %collective-permute-done.6.args_3_, ...), custom_call_target="tpu_custom_call" | custom-call | flops 603979776 | bytes 2359296 | tf_op jit(solution)/shard_map/jump/pallas_call | solution.py:285
  70.8 6.6 %collective-permute-start.10 = (bf16[80,768]{1,0:T(8,128)(2,1)S(1)}, bf16[80,768]{1,0:T(8,128)(2,1)S(1)}, u32[]{:S(2)}, u32[]{:S(2)}) collective-permute-start(bf16[80,768]{1,0:T(8,128)(2,1)S(1)} %get-tuple-element.21), channel_id=1, source_target_pairs={{120,96},{248,224},{376,352},{128,152},{256,280},{384,408},{121,97... | collective-permute-start | bytes 368648 | tf_op jit(solution)/shard_map/ppermute | solution.py:253
  77.4 1.3 collective-permute-start.12
  78.7 0.0 copy-start.2
  78.7 10.9 %collective-permute-start.9 = (bf16[112,768]{1,0:T(8,128)(2,1)S(1)}, bf16[112,768]{1,0:T(8,128)(2,1)S(1)}, u32[]{:S(2)}, u32[]{:S(2)}) collective-permute-start(bf16[112,768]{1,0:T(8,128)(2,1)S(1)} %get-tuple-element.20), channel_id=1, source_target_pairs={{120,128},{248,256},{376,384},{128,120},{256,248},{384,376},{121,1... | collective-permute-start | bytes 516104 | tf_op jit(solution)/shard_map/ppermute | solution.py:253
  89.6 0.0 collective-permute-done.10
  89.6 1.3 collective-permute-start.11
  90.9 0.0 collective-permute-done.12
  90.9 1.3 collective-permute-start.13
  92.2 6.4 %own.1 = (f32[256,768]{1,0:T(8,128)S(1)}, f32[256,128]{1,0:T(8,128)S(1)}) custom-call(s32[128,4]{1,0:T(8,128)S(1)} %copy.17.pattern_ref.args_0_, s32[128]{0:T(128)S(1)} %copy-done.3, bf16[256,768]{1,0:T(8,128)(2,1)S(1)} %bitcast.31, bf16[8,2,32,768]{3,2,1,0:T(8,128)(2,1)S(1)} %all-to-all-done.1.kv_ref.args_5_, bf16[512,768]{1,0:T(8,128)(2,1)S(1)} %copy-done, ...), custom_call_target="tpu_custom_call" | custom-call | flops 603979776 | bytes 2359296 | tf_op jit(solution)/shard_map/own/pallas_call | solution.py:296
  98.7 6.6 %collective-permute-done.9.part0_ref = bf16[112,768]{1,0:T(8,128)(2,1)S(1)} collective-permute-done((bf16[112,768]{1,0:T(8,128)(2,1)S(1)}, bf16[112,768]{1,0:T(8,128)(2,1)S(1)}, u32[]{:S(2)}, u32[]{:S(2)}) %collective-permute-start.9) | collective-permute-done | bytes 172064 | tf_op jit(solution)/shard_map/ppermute | solution.py:253
  105.3 3.1 %collective-permute-done.11.part1_ref = bf16[80,768]{1,0:T(8,128)(2,1)S(1)} collective-permute-done((bf16[80,768]{1,0:T(8,128)(2,1)S(1)}, bf16[80,768]{1,0:T(8,128)(2,1)S(1)}, u32[]{:S(2)}, u32[]{:S(2)}) %collective-permute-start.11) | collective-permute-done | bytes 122912 | tf_op jit(solution)/shard_map/ppermute | solution.py:253
  108.5 3.5 %collective-permute-done.13.part2_ref = bf16[80,768]{1,0:T(8,128)(2,1)S(1)} collective-permute-done((bf16[80,768]{1,0:T(8,128)(2,1)S(1)}, bf16[80,768]{1,0:T(8,128)(2,1)S(1)}, u32[]{:S(2)}, u32[]{:S(2)}) %collective-permute-start.13) | collective-permute-done | bytes 122912 | tf_op jit(solution)/shard_map/ppermute | solution.py:253
  111.9 0.0 collective-permute-done.2.low_ref
  111.9 0.0 collective-permute-done.3.high_ref
  111.9 0.0 copy-done.2
  111.9 0.8 mix.1
  112.8 18.2 %all_to_all.15 = bf16[8,32,768]{2,1,0:T(8,128)(2,1)S(1)} all-to-all(bf16[8,32,768]{2,1,0:T(8,128)(2,1)S(1)} %bitcast.32), channel_id=1, replica_groups=mesh['ctx'=64,'head'=8] {'head'}, dimensions={0} | all-to-all | bytes 786432 | tf_op jit(solution)/shard_map/all_to_all | solution.py:317
  131.0 0.8 copy.24
  (2 shorter events, 0.0 us)
Async XLA Ops:
  1.8 6.0 %copy-start.4 = (bf16[32,6144]{1,0:T(8,128)(2,1)S(1)}, bf16[32,6144]{1,0:T(8,128)(2,1)}, u32[]{:S(2)}) copy-start(bf16[32,6144]{1,0:T(8,128)(2,1)} %param.10) | copy-start | bytes 1179652
  1.8 6.0 %copy-start.5 = (bf16[32,6144]{1,0:T(8,128)(2,1)S(1)}, bf16[32,6144]{1,0:T(8,128)(2,1)}, u32[]{:S(2)}) copy-start(bf16[32,6144]{1,0:T(8,128)(2,1)} %param.9) | copy-start | bytes 1179652
  1.8 18.6 %all-to-all-start = ((bf16[8,32,768]{2,1,0:T(8,128)(2,1)}), bf16[8,32,768]{2,1,0:T(8,128)(2,1)S(1)}, u32[]{:S(2)}, u32[]{:S(2)}) async-start(bf16[8,32,768]{2,1,0:T(8,128)(2,1)} %bitcast.26), calls=%async_computation | async-start | bytes 786432 | tf_op jit(solution)/shard_map/all_to_all | solution.py:258
  20.3 15.9 %copy-start.6 = (s32[128,4]{0,1:T(4,128)S(1)}, s32[128,4]{0,1:T(4,128)}, u32[]{:S(2)}) copy-start(s32[128,4]{0,1:T(4,128)} %param.13) | copy-start | bytes 6148
  20.3 29.9 %copy-start.1 = (bf16[512,768]{1,0:T(8,128)(2,1)S(1)}, bf16[512,768]{1,0:T(8,128)(2,1)}, u32[]{:S(2)}) copy-start(bf16[512,768]{1,0:T(8,128)(2,1)} %args_7_.4) | copy-start | bytes 2359300
  20.3 29.9 %all-to-all-start.1 = ((bf16[8,2,32,768]{3,2,1,0:T(8,128)(2,1)}), bf16[8,2,32,768]{3,2,1,0:T(8,128)(2,1)S(1)}, u32[]{:S(2)}, u32[]{:S(2)}) async-start(bf16[8,2,32,768]{3,2,1,0:T(8,128)(2,1)} %pad_maximum_fusion), calls=%async_computation.1 | async-start | bytes 1572864 | tf_op jit(solution)/shard_map/all_to_all | solution.py:265
  24.0 26.2 %copy-start = (bf16[512,768]{1,0:T(8,128)(2,1)S(1)}, bf16[512,768]{1,0:T(8,128)(2,1)}, u32[]{:S(2)}) copy-start(bf16[512,768]{1,0:T(8,128)(2,1)} %args_6_.4) | copy-start | bytes 2359300
  24.0 26.2 %collective-permute-start = (bf16[256,768]{1,0:T(8,128)(2,1)S(1)}, bf16[256,768]{1,0:T(8,128)(2,1)}, u32[]{:S(2)}, u32[]{:S(2)}) collective-permute-start(bf16[256,768]{1,0:T(8,128)(2,1)S(1)} %bitcast.27), channel_id=1, source_target_pairs={{0,8},{8,16},{16,24},{24,32},{32,40},{40,48},{48,56},{56,64},{64,7... | collective-permute-start | bytes 1179656 | tf_op jit(solution)/shard_map/ppermute | solution.py:253
  25.5 24.8 %collective-permute-start.1 = (bf16[256,768]{1,0:T(8,128)(2,1)S(1)}, bf16[256,768]{1,0:T(8,128)(2,1)}, u32[]{:S(2)}, u32[]{:S(2)}) collective-permute-start(bf16[256,768]{1,0:T(8,128)(2,1)S(1)} %bitcast.28), channel_id=1, source_target_pairs={{8,0},{16,8},{24,16},{32,24},{40,32},{48,40},{56,48},{64,56},{72,6... | collective-permute-start | bytes 1179656 | tf_op jit(solution)/shard_map/ppermute | solution.py:253
  30.8 16.8 %collective-permute-start.5 = (bf16[80,768]{1,0:T(8,128)(2,1)S(1)}, bf16[80,768]{1,0:T(8,128)(2,1)S(1)}, u32[]{:S(2)}, u32[]{:S(2)}) collective-permute-start(bf16[80,768]{1,0:T(8,128)(2,1)S(1)} %get-tuple-element.24), channel_id=1, source_target_pairs={{120,96},{248,224},{376,352},{128,152},{256,280},{384,408},{121,97... | collective-permute-start | bytes 368648 | tf_op jit(solution)/shard_map/ppermute | solution.py:253
  34.3 14.6 %collective-permute-start.7 = (bf16[80,768]{1,0:T(8,128)(2,1)S(1)}, bf16[80,768]{1,0:T(8,128)(2,1)}, u32[]{:S(2)}, u32[]{:S(2)}) collective-permute-start(bf16[80,768]{1,0:T(8,128)(2,1)S(1)} %get-tuple-element.23), channel_id=1, source_target_pairs={{120,24},{248,152},{376,280},{128,224},{256,352},{384,480},{121,25... | collective-permute-start | bytes 368648 | tf_op jit(solution)/shard_map/ppermute | solution.py:253
  36.4 13.9 %copy-start.3 = (s32[128]{0:T(128)S(1)}, s32[128]{0:T(128)}, u32[]{:S(2)}) copy-start(s32[128]{0:T(128)} %args_1_.4) | copy-start | bytes 1540
  36.4 29.4 %collective-permute-start.4 = (bf16[96,768]{1,0:T(8,128)(2,1)S(1)}, bf16[96,768]{1,0:T(8,128)(2,1)S(1)}, u32[]{:S(2)}, u32[]{:S(2)}) collective-permute-start(bf16[96,768]{1,0:T(8,128)(2,1)S(1)} %slice.9), channel_id=1, source_target_pairs={{120,128},{248,256},{376,384},{128,120},{256,248},{384,376},{121,1... | collective-permute-start | bytes 442376 | tf_op jit(solution)/shard_map/ppermute | solution.py:253
  47.6 18.2 %collective-permute-start.6 = (bf16[80,768]{1,0:T(8,128)(2,1)S(1)}, bf16[80,768]{1,0:T(8,128)(2,1)S(1)}, u32[]{:S(2)}, u32[]{:S(2)}) collective-permute-start(bf16[80,768]{1,0:T(8,128)(2,1)S(1)} %collective-permute-done.5), channel_id=1, source_target_pairs={{96,128},{224,256},{352,384},{152,120},{280,248},{408,376},{97,129... | collective-permute-start | bytes 368648 | tf_op jit(solution)/shard_map/ppermute | solution.py:253
  48.9 16.9 %collective-permute-start.8 = (bf16[80,768]{1,0:T(8,128)(2,1)}, bf16[80,768]{1,0:T(8,128)(2,1)S(1)}, u32[]{:S(2)}, u32[]{:S(2)}) collective-permute-start(bf16[80,768]{1,0:T(8,128)(2,1)} %collective-permute-done.7), channel_id=1, source_target_pairs={{24,128},{152,256},{280,384},{224,120},{352,248},{480,376},{25,129... | collective-permute-start | bytes 368648 | tf_op jit(solution)/shard_map/ppermute | solution.py:253
  56.2 55.7 %collective-permute-start.2 = (bf16[272,768]{1,0:T(8,128)(2,1)S(1)}, bf16[272,768]{1,0:T(8,128)(2,1)S(1)}, u32[]{:S(2)}, u32[]{:S(2)}) collective-permute-start(bf16[272,768]{1,0:T(8,128)(2,1)S(1)} %get-tuple-element.18), channel_id=1, source_target_pairs={{0,8},{8,16},{16,24},{24,32},{32,40},{40,48},{48,56},{56,64},{64,7... | collective-permute-start | bytes 1253384 | tf_op jit(solution)/shard_map/ppermute | solution.py:253
  57.5 54.4 %collective-permute-start.3 = (bf16[272,768]{1,0:T(8,128)(2,1)S(1)}, bf16[272,768]{1,0:T(8,128)(2,1)S(1)}, u32[]{:S(2)}, u32[]{:S(2)}) collective-permute-start(bf16[272,768]{1,0:T(8,128)(2,1)S(1)} %get-tuple-element.19), channel_id=1, source_target_pairs={{8,0},{16,8},{24,16},{32,24},{40,32},{48,40},{56,48},{64,56},{72,6... | collective-permute-start | bytes 1253384 | tf_op jit(solution)/shard_map/ppermute | solution.py:253
  70.8 18.8 %collective-permute-start.10 = (bf16[80,768]{1,0:T(8,128)(2,1)S(1)}, bf16[80,768]{1,0:T(8,128)(2,1)S(1)}, u32[]{:S(2)}, u32[]{:S(2)}) collective-permute-start(bf16[80,768]{1,0:T(8,128)(2,1)S(1)} %get-tuple-element.21), channel_id=1, source_target_pairs={{120,96},{248,224},{376,352},{128,152},{256,280},{384,408},{121,97... | collective-permute-start | bytes 368648 | tf_op jit(solution)/shard_map/ppermute | solution.py:253
  77.4 13.5 %collective-permute-start.12 = (bf16[80,768]{1,0:T(8,128)(2,1)S(1)}, bf16[80,768]{1,0:T(8,128)(2,1)S(1)}, u32[]{:S(2)}, u32[]{:S(2)}) collective-permute-start(bf16[80,768]{1,0:T(8,128)(2,1)S(1)} %get-tuple-element.22), channel_id=1, source_target_pairs={{120,24},{248,152},{376,280},{128,224},{256,352},{384,480},{121,25... | collective-permute-start | bytes 368648 | tf_op jit(solution)/shard_map/ppermute | solution.py:253
  78.7 33.2 %copy-start.2 = (f32[6144]{0:T(1024)S(1)}, f32[6144]{0:T(1024)}, u32[]{:S(2)}) copy-start(f32[6144]{0:T(1024)} %param.15) | copy-start | bytes 73732
  78.7 26.6 %collective-permute-start.9 = (bf16[112,768]{1,0:T(8,128)(2,1)S(1)}, bf16[112,768]{1,0:T(8,128)(2,1)S(1)}, u32[]{:S(2)}, u32[]{:S(2)}) collective-permute-start(bf16[112,768]{1,0:T(8,128)(2,1)S(1)} %get-tuple-element.20), channel_id=1, source_target_pairs={{120,128},{248,256},{376,384},{128,120},{256,248},{384,376},{121,1... | collective-permute-start | bytes 516104 | tf_op jit(solution)/shard_map/ppermute | solution.py:253
  89.6 18.8 %collective-permute-start.11 = (bf16[80,768]{1,0:T(8,128)(2,1)S(1)}, bf16[80,768]{1,0:T(8,128)(2,1)S(1)}, u32[]{:S(2)}, u32[]{:S(2)}) collective-permute-start(bf16[80,768]{1,0:T(8,128)(2,1)S(1)} %collective-permute-done.10), channel_id=1, source_target_pairs={{96,128},{224,256},{352,384},{152,120},{280,248},{408,376},{97,129... | collective-permute-start | bytes 368648 | tf_op jit(solution)/shard_map/ppermute | solution.py:253
  90.9 21.0 %collective-permute-start.13 = (bf16[80,768]{1,0:T(8,128)(2,1)S(1)}, bf16[80,768]{1,0:T(8,128)(2,1)S(1)}, u32[]{:S(2)}, u32[]{:S(2)}) collective-permute-start(bf16[80,768]{1,0:T(8,128)(2,1)S(1)} %collective-permute-done.12), channel_id=1, source_target_pairs={{24,128},{152,256},{280,384},{224,120},{352,248},{480,376},{25,129... | collective-permute-start | bytes 368648 | tf_op jit(solution)/shard_map/ppermute | solution.py:253
